TPU v7x, 128 devices: a whole 4x4x4 slice. The times are simulated.
128 devices in a mesh: ctx: 16 (over z_hi, x, core), hx: 8 (over y, z_lo).
Axes of the slice: x: 4, y: 4, z: 4 (z_hi: 2, z_lo: 2; z = z_hi * 2 + z_lo), core: 2. Of those that a mesh axis runs over, the one named last changes fastest.
Arguments:
- tokens: bfloat16 [8192, 5120], P('ctx'), may hold values from -6 to 6
- attn_gain: bfloat16 [5120], replicated, may hold values from 0.5 to 1.5
- ffn_gain: bfloat16 [5120], replicated, may hold values from 0.5 to 1.5
- w_query: bfloat16 [5120, 3072], P('ctx', 'hx'), may hold values from -3 to 3
- w_key: bfloat16 [5120, 1024], P('ctx', 'hx'), may hold values from -1 to 1
- w_value: bfloat16 [5120, 1024], P('ctx', 'hx'), may hold values from -0.078125 to 0.078125
- w_out: bfloat16 [3072, 5120], P('hx'), may hold values from -0.109375 to 0.109375
- w_router: bfloat16 [5120, 16], replicated, may hold values from -0.078125 to 0.078125
- routes: int32 [8192, 1], P('ctx'), may hold values from 0 to 15; in each aligned block of 512 rows (0 to 511, 512 to 1023, ...) at most 64 rows name the same one
- w_gate: bfloat16 [16, 5120, 4096], P('ctx', None, 'hx'), may hold values from -0.078125 to 0.078125
- w_up: bfloat16 [16, 5120, 4096], P('ctx', None, 'hx'), may hold values from -0.078125 to 0.078125
- w_down: bfloat16 [16, 4096, 5120], P('ctx', 'hx'), may hold values from -0.09375 to 0.09375
Outputs:
- layer_out: bfloat16 [8192, 5120], P('ctx', 'hx')
Inputs may be any that keep to these rules, and one draw needn't show every extreme that they name: `routes`: within the 512 rows of one device, no expert is named by more than 64 rows, a bound that some block reaches.
All inputs are finite; a program needn't handle non-finite values.
Results may differ from a plain program's by a relative error of at most 0.0095.
Values may be sent and summed in bfloat16 or wider, within the bound.
A program may use at most 128 MiB of HBM per device.

v0:
```python
import jax
import jax.numpy as jnp
from jax import lax
from jax.sharding import Mesh
from jax.sharding import PartitionSpec as P

HD = 128
HX = ("hx_0", "hx_1")


epsilon = 1e-05
block_rows = 1024


def side_by_side(arrays, axis, dim, along):
    ends, at = ([], 0)
    for a in arrays[:-1]:
        at += a.shape[along]
        ends.append(at)
    both = jnp.concatenate(arrays, axis=along)
    return tuple(jnp.split(lax.all_gather(both, axis, axis=dim, tiled=True), ends, axis=along))


def summed_rows(x, axes, dim):
    if not axes:
        return x
    nearer = lax.psum_scatter(x, axes[0], scatter_dimension=dim, tiled=True)
    return summed_rows(nearer, axes[1:], dim)


def root_norm(values, gains):
    floats = values.astype(jnp.float32)
    inverse = lax.rsqrt(jnp.mean(floats * floats, axis=-1, keepdims=True) + epsilon)
    return (floats * inverse * gains.astype(jnp.float32)).astype(jnp.bfloat16)


def body(
    tokens,
    attn_gain,
    ffn_gain,
    w_query,
    w_key,
    w_value,
    w_out,
    w_router,
    routes,
    w_gate,
    w_up,
    w_down,
):
    ctx_count = lax.axis_size("ctx")
    hx_count = lax.axis_size(HX)
    hx_index = lax.axis_index(HX)
    tok_rows = tokens.shape[0]
    full_width = tokens.shape[1]
    local_width = full_width // hx_count
    normed = root_norm(tokens, attn_gain)
    pieces = side_by_side((w_query, w_key, w_value), "ctx", 0, 1)
    queries, key_proj, value_proj = tuple(
        (jnp.dot(normed, matrix, preferred_element_type=jnp.float32) for matrix in pieces)
    )
    kv_heads = key_proj.shape[1] // HD
    group_size = queries.shape[1] // HD // kv_heads
    queries_all = queries.astype(jnp.bfloat16).reshape(tok_rows, kv_heads, group_size, HD)
    key_local = key_proj.astype(jnp.bfloat16)
    value_local = value_proj.astype(jnp.bfloat16)
    query_first = lax.axis_index("ctx") * tok_rows
    query_pos = query_first + jnp.arange(tok_rows, dtype=jnp.int32)

    def attend(running, key_block, value_block, key_start):
        running_max, running_sum, running_out = running
        count_here = key_block.shape[0]
        key_heads = key_block.reshape(count_here, kv_heads, HD)
        value_heads = value_block.reshape(count_here, kv_heads, HD)
        scores = jnp.einsum(
            "tkgd,skd->tkgs", queries_all, key_heads, preferred_element_type=jnp.float32
        ) * HD ** (-0.5)
        key_pos = key_start + jnp.arange(count_here, dtype=jnp.int32)
        visible = (key_pos[None, :] <= query_pos[:, None])[:, None, None, :]
        masked = jnp.where(visible, scores, -jnp.inf)
        new_max = jnp.maximum(running_max, jnp.max(masked, axis=-1))
        weights = jnp.where(visible, jnp.exp(scores - new_max[..., None]), 0.0)
        factor = jnp.exp(running_max - new_max)
        new_sum = running_sum * factor + jnp.sum(weights, axis=-1)
        contrib = jnp.einsum(
            "tkgs,skd->tkgd",
            weights.astype(jnp.bfloat16),
            value_heads,
            preferred_element_type=jnp.float32,
        )
        return (new_max, new_sum, running_out * factor[..., None] + contrib)

    def visit(running, key_block, value_block, key_start):
        return attend(running, key_block, value_block, key_start)

    start_max = jnp.full((tok_rows, kv_heads, group_size), -1e30, jnp.float32)
    start_sum = jnp.zeros((tok_rows, kv_heads, group_size), jnp.float32)
    start_out = jnp.zeros((tok_rows, kv_heads, group_size, HD), jnp.float32)
    key_rows, value_rows = side_by_side((key_local, value_local), "ctx", 0, 1)
    count_all = key_rows.shape[0]

    def block_step(block_index, held):
        inner = block_index * block_rows
        key_block = lax.dynamic_slice_in_dim(key_rows, inner, block_rows, 0)
        value_block = lax.dynamic_slice_in_dim(value_rows, inner, block_rows, 0)
        return visit(held, key_block, value_block, inner)

    final_max, final_sum, final_out = lax.fori_loop(
        0, count_all // block_rows, block_step, (start_max, start_sum, start_out)
    )
    attended = (final_out / final_sum[..., None]).astype(jnp.bfloat16).reshape(tok_rows, -1)
    partial_attn = jnp.dot(attended, w_out, preferred_element_type=jnp.float32)
    share_sum = lax.psum_scatter(
        partial_attn.astype(jnp.bfloat16), HX, scatter_dimension=1, tiled=True
    ).astype(jnp.float32)
    own_tokens = lax.dynamic_slice_in_dim(tokens, hx_index * local_width, local_width, 1)
    own_stream = (own_tokens.astype(jnp.float32) + share_sum).astype(jnp.bfloat16)
    stream = lax.all_gather(own_stream, HX, axis=1, tiled=True)
    normed2 = root_norm(stream, ffn_gain)
    logits = jnp.dot(normed2, w_router, preferred_element_type=jnp.float32)
    expert_count = w_router.shape[1]
    chosen = routes[:, 0]
    onehot = chosen[:, None] == jnp.arange(expert_count, dtype=jnp.int32)[None, :]
    router_score = jax.nn.sigmoid(jnp.sum(jnp.where(onehot, logits, 0.0), axis=-1))
    routed = (normed2.astype(jnp.float32) * router_score[:, None]).astype(jnp.bfloat16)
    counts = jnp.cumsum(onehot.astype(jnp.int32), axis=0)
    position = jnp.sum(jnp.where(onehot, counts, 0), axis=-1) - 1
    capacity = tok_rows // 8
    slot_index = chosen * capacity + position
    exp_local = w_gate.shape[0]
    routed_share = lax.dynamic_slice_in_dim(routed, hx_index * local_width, local_width, 1)
    buffer = (
        jnp.zeros((expert_count * capacity, local_width), jnp.bfloat16)
        .at[slot_index]
        .set(routed_share)
    )
    buffer = buffer.reshape(ctx_count, exp_local, capacity, local_width)
    arrived = lax.all_to_all(buffer, "ctx", split_axis=0, concat_axis=0, tiled=True)
    joined = lax.all_gather(arrived, HX, axis=3, tiled=True)
    gate_out = jnp.einsum("secd,edf->secf", joined, w_gate, preferred_element_type=jnp.float32)
    up_out = jnp.einsum("secd,edf->secf", joined, w_up, preferred_element_type=jnp.float32)
    hidden = (jax.nn.silu(gate_out) * up_out).astype(jnp.bfloat16)
    partial_expert = jnp.einsum(
        "secf,efd->secd", hidden, w_down, preferred_element_type=jnp.float32
    )
    reduced = (
        summed_rows(partial_expert.astype(jnp.bfloat16), HX, 3)
        .astype(jnp.float32)
        .astype(jnp.bfloat16)
    )
    returned = lax.all_to_all(reduced, "ctx", split_axis=0, concat_axis=0, tiled=True)
    flat_rows = returned.reshape(expert_count * capacity, local_width)
    expert_out = flat_rows[slot_index]
    return (own_stream.astype(jnp.float32) + expert_out.astype(jnp.float32)).astype(jnp.bfloat16)


def solution(mesh):
    finer = Mesh(mesh.devices.reshape(mesh.shape["ctx"], 4, 2), ("ctx", "hx_0", "hx_1"))
    in_specs = (
        P("ctx", None),
        P(),
        P(),
        P("ctx", HX),
        P("ctx", HX),
        P("ctx", HX),
        P(HX, None),
        P(),
        P("ctx", None),
        P("ctx", None, HX),
        P("ctx", None, HX),
        P("ctx", HX, None),
    )
    out_specs = P("ctx", HX)
    return jax.shard_map(body, mesh=finer, in_specs=in_specs, out_specs=out_specs, check_vma=False)
```

profile of v0, /device:TPU:1, one launch (start us, length us, event | category | flops | bytes accessed | tf_op | source)
XLA Modules:
  0.0 904.5 jit_solution(17988157199524055893)
XLA Ops:
  9.2 3.6 fusion.28
  12.8 65.6 %all-gather.5.cloned.1.call-done = bf16[5120,640]{1,0:T(8,128)(2,1)} async-done(((bf16[320,640]{1,0:T(8,128)(2,1)}), bf16[5120,640]{1,0:T(8,128)(2,1)}) %all-gather.5.cloned.1.call-update) | async-done | bytes 6553616 | tf_op jit(solution)/shard_map/all_gather | solution.py:21
  78.3 4.8 fusion.66
  83.2 4.8 fusion.63
  89.0 6.1 fusion.60
  95.3 50.5 %all-gather.7.cloned.1.call-done = bf16[8192,256]{0,1:T(8,128)(2,1)} async-done(((bf16[512,256]{0,1:T(8,128)(2,1)}), bf16[8192,256]{0,1:T(8,128)(2,1)}) %all-gather.7.cloned.1.call-update) | async-done | bytes 4194320 | tf_op jit(solution)/shard_map/all_gather | solution.py:21
  145.8 3.9 fusion.80
  149.8 47.9 %while.18 = (s32[]{:T(128)}, f32[512,1,3]{0,2,1:T(4,128)S(1)}, f32[512,1,3]{0,2,1:T(4,128)S(1)}, f32[512,1,3,128]{0,3,2,1:T(8,128)S(1)}, bf16[8192,128]{0,1:T(8,...) while((s32[]{:T(128)}, f32[512,1,3]{0,2,1:T(4,128)S(1)}, ...), condition=%wide.region_4.5_spmd.clone, body=%wide.region_1.4_spmd.clone.sunk | while | flops 823732736 | bytes 23572680 | solution.py:108
  152.9 2.8 fusion.97
  158.9 2.8 fusion.97
  170.9 2.8 fusion.97
  182.9 2.8 fusion.97
  194.9 2.8 fusion.97
  197.8 6.8 convolution_convert_fusion
  204.6 7.9 copy.28
  212.7 108.1 %reduce-scatter.10.cloned.1.call-done = bf16[640,512]{1,0:T(8,128)(2,1)} async-done(((bf16[5120,512]{1,0:T(8,128)(2,1)}), bf16[640,512]{1,0:T(8,128)(2,1)}) %reduce-scatter.10.cloned.1.call-update) | async-done | bytes 655376
  326.1 108.5 %all-gather.9.cloned.1.call-done = bf16[512,5120]{1,0:T(8,128)(2,1)} async-done(((bf16[512,640]{1,0:T(8,128)(2,1)}), bf16[512,5120]{1,0:T(8,128)(2,1)}) %all-gather.9.cloned.1.call-update) | async-done | bytes 5242896 | tf_op jit(solution)/shard_map/all_gather | solution.py:118
  434.7 3.7 fusion.31
  444.5 3.5 scatter_custom_fusion
  448.0 27.2 %all_to_all.10 = bf16[16,1,64,640]{3,2,1,0:T(8,128)(2,1)} all-to-all(bf16[16,1,64,640]{3,2,1,0:T(8,128)(2,1)S(1)} %bitcast.185), channel_id=1, replica_groups=mesh['ctx'=16,'hx_0'=4,'hx_1'=2] {'ctx'}, dimensions={0} | all-to-all | bytes 2621440 | tf_op jit(solution)/shard_map/all_to_all | solution.py:138
  475.6 204.2 %all-gather.11.cloned.1.call-done = bf16[16,1,64,5120]{3,2,0,1:T(8,128)(2,1)} async-done(((bf16[16,1,64,640]{3,2,0,1:T(8,128)(2,1)}), bf16[16,1,64,5120]{3,2,0,1:T(8,128)(2,1)}) %all-gather.11.cloned.1.call-update) | async-done | bytes 10485776 | tf_op jit(solution)/shard_map/all_gather | solution.py:139
  679.8 9.9 %fusion.36 = f32[16,64,512]{2,1,0:T(8,128)S(1)} fusion(bf16[16,1,64,5120]{3,2,0,1:T(8,128)(2,1)} %all-gather.11.cloned.1.call-done, bf16[1,5120,512]{2,1,0:T(8,128)(2,1)} %param.23), kind=kOutput, calls=%fused_computation.46 | convolution fusion | flops 5368709120 | bytes 17825792 | tf_op jit(solution)/shard_map/secd,edf->secf/dot_general | solution.py:140
  689.8 7.7 fusion.51
  697.6 8.2 convert_bitcast_fusion
  705.9 98.7 %reduce-scatter.8.cloned.1.call-done = bf16[16,1,64,1280]{3,2,0,1:T(8,128)(2,1)} async-done(((bf16[16,1,64,5120]{3,2,0,1:T(8,128)(2,1)}), bf16[16,1,64,1280]{3,2,0,1:T(8,128)(2,1)}) %reduce-scatter.8.cloned.1.call-update) | async-done | bytes 2621456 | tf_op jit(solution)/shard_map/reduce_scatter | solution.py:27
  804.5 7.5 copy.30
  812.1 7.9 reshape.196
  820.0 40.0 %reduce-scatter.12.cloned.1.call-done = bf16[640,1024]{1,0:T(8,128)(2,1)} async-done(((bf16[1280,1024]{1,0:T(8,128)(2,1)}), bf16[640,1024]{1,0:T(8,128)(2,1)}) %reduce-scatter.12.cloned.1.call-update) | async-done | bytes 1310736
  860.0 3.4 reshape.197
  863.4 3.7 copy.31
  867.0 7.5 all-to-all-start.1
  874.6 20.1 %all-to-all-done.1 = bf16[16,1,64,640]{3,2,1,0:T(8,128)(2,1)S(1)} async-done(((bf16[16,1,64,640]{3,2,1,0:T(8,128)(2,1)}), bf16[16,1,64,640]{3,2,1,0:T(8,128)(2,1)S(1)}, u32[]{:S(2)}, u32[]{:S(2)}) %all-to-all-start.1) | async-done | bytes 1310752 | tf_op jit(solution)/shard_map/all_to_all | solution.py:151
  (127 shorter events, 52.2 us)
Async XLA Ops:
  6.5 436.5 %copy-start = (bf16[5120,16]{0,1:T(8,128)(2,1)S(1)}, bf16[5120,16]{0,1:T(8,128)(2,1)}, u32[]{:S(2)}) copy-start(bf16[5120,16]{0,1:T(8,128)(2,1)} %param.21) | copy-start | bytes 491524
  6.5 71.8 %all-gather.5.cloned.1.call-start = ((), (), s32[]{:S(2)}) async-start(), calls=%async_computation.5 | async-start | bytes 6963200 | tf_op jit(solution)/shard_map/all_gather | solution.py:21
  8.4 137.4 %all-gather.7.cloned.1.call-start = ((), (), s32[]{:S(2)}) async-start(), calls=%async_computation.6 | async-start | bytes 4456448 | tf_op jit(solution)/shard_map/all_gather | solution.py:21
  88.8 232.0 %reduce-scatter.10.cloned.1.call-start = ((), (), s32[]{:S(2)}) async-start(), calls=%async_computation.10 | async-start | bytes 5898240
  212.6 112.0 %copy-start.5 = (bf16[5120]{0:T(1024)(128)(2,1)S(1)}, bf16[5120]{0:T(1024)(128)(2,1)}, u32[]{:S(2)}) copy-start(bf16[5120]{0:T(1024)(128)(2,1)} %param.16) | copy-start | bytes 30724
  212.6 112.0 %copy-start.4 = (s32[512,1]{0,1:T(1,128)S(1)}, s32[512,1]{0,1:T(1,128)}, u32[]{:S(2)}) copy-start(s32[512,1]{0,1:T(1,128)} %param.22) | copy-start | bytes 6148
  212.6 222.1 %all-gather.9.cloned.1.call-start = ((), (), s32[]{:S(2)}) async-start(), calls=%async_computation.7 | async-start | bytes 5898240 | tf_op jit(solution)/shard_map/all_gather | solution.py:118
  324.3 355.6 %all-gather.11.cloned.1.call-start = ((), (), s32[]{:S(2)}) async-start(), calls=%async_computation.8 | async-start | bytes 11796480 | tf_op jit(solution)/shard_map/all_gather | solution.py:139
  434.7 4.0 copy-start.2
  440.7 2.3 copy-start.1
  475.3 329.2 %reduce-scatter.8.cloned.1.call-start = ((), (), s32[]{:S(2)}) async-start(), calls=%async_computation.9 | async-start | bytes 13107200 | tf_op jit(solution)/shard_map/reduce_scatter | solution.py:27
  679.8 10.0 %copy-start.6 = (bf16[16,1,64,5120]{3,2,0,1:T(8,128)(2,1)S(1)}, bf16[16,1,64,5120]{3,2,0,1:T(8,128)(2,1)}, u32[]{:S(2)}) copy-start(bf16[16,1,64,5120]{3,2,0,1:T(8,128)(2,1)} %all-gather.11.cloned.1.call-done) | copy-start | bytes 31457284
  679.8 17.7 %slice-start = ((s8[5242880]{0:T(1024)(128)(4,1)}), s8[4194304]{0:T(1024)(128)(4,1)S(1)}, s32[]{:S(2)}) async-start(s8[5242880]{0:T(1024)(128)(4,1)} %bitcast.199), calls=%async_computation.12 | async-start | bytes 8388608
  689.8 7.8 slice-start.1
  705.8 154.2 %reduce-scatter.12.cloned.1.call-start = ((), (), s32[]{:S(2)}) async-start(), calls=%async_computation.11 | async-start | bytes 3932160
  867.0 29.6 %copy-start.3 = (bf16[512,640]{1,0:T(8,128)(2,1)S(1)}, bf16[512,640]{1,0:T(8,128)(2,1)}, u32[]{:S(2)}) copy-start(bf16[512,640]{1,0:T(8,128)(2,1)} %add_convert_fusion.1) | copy-start | bytes 1966084
  867.0 27.6 %all-to-all-start.1 = ((bf16[16,1,64,640]{3,2,1,0:T(8,128)(2,1)}), bf16[16,1,64,640]{3,2,1,0:T(8,128)(2,1)S(1)}, u32[]{:S(2)}, u32[]{:S(2)}) async-start(bf16[16,1,64,640]{3,2,1,0:T(8,128)(2,1)} %bitcast.186), calls=%async_computation.2 | async-start | bytes 2621440 | tf_op jit(solution)/shard_map/all_to_all | solution.py:151
Sparse Core Ops, SparseCore 0:
  9.8 68.5 all-gather.4
  88.9 56.9 all-gather.6
  212.7 108.0 reduce-scatter.9
  324.4 110.2 all-gather.8
  475.4 204.3 all-gather.10
  705.9 98.5 reduce-scatter.7
  820.1 39.8 reduce-scatter.11
where the time goes:
time: 906 us; the launch traced here: 905 us
  waiting for transfers between devices  696 us (77%)
  matrix products  83 us (9%)
  local copies, waits for them, and re-layouts  40.8 us (5%)
  other arithmetic  34.8 us (4%)
  blocking collectives  27.2 us (3%)
  between operations  13.8 us (2%)
    all_gather x1, waiting for transfers between devices, body(): joined = lax.all_gather(arrived, HX, axis=3, tiled=True)  204 us
    unnamed x9, waiting for transfers between devices  148 us
    all_gather x2, waiting for transfers between devices, side_by_side(): lax.all_gather(both, axis, axis=dim, tiled=True)  116 us
    all_gather x1, waiting for transfers between devices, body(): stream = lax.all_gather(own_stream, HX, axis=1, tiled=True)  109 us
    reduce_scatter x1, waiting for transfers between devices, summed_rows(): nearer = lax.psum_scatter(x, axes[0], scatter_dimension=dim, tiled=True)  98.7 us
    unnamed x25, local copies, waits for them, and re-layouts  34.6 us
    all_to_all x1, blocking collectives, body(): lax.all_to_all(buffer, 'ctx', split_axis=0, concat_axis=0, tiled=True)  27.2 us
    dot_general x8, matrix products, attend(): jnp.einsum('tkgs,skd->tkgd', weights.astype(jnp.bfloat16), value_heads, p...  22.3 us
  transfers between devices with their start and end apart: 8, of which 8 were waited for; matrix products, arithmetic and copies ran while one was open for 1% of the time, Pallas kernels for 0%

commit v1 on v0

v1 whole, which is shorter than its diff:
```python
import functools
import math
import jax
import jax.numpy as jnp
from jax import lax
from jax.experimental import pallas as pl
from jax.experimental.pallas import tpu as pltpu
from jax.sharding import PartitionSpec as P

HD = 128
epsilon = 1e-05
MESH = pl.DeviceIdType.MESH


def place():
    ctx, hx = lax.axis_index("ctx"), lax.axis_index("hx")
    z_hi, x, core = ctx // 8, (ctx // 2) % 4, ctx % 2
    y, z_lo = hx // 2, hx % 2
    return z_hi, x, core, y, z_lo


def ctx_of(z_hi, x, core):
    return z_hi * 8 + x * 2 + core


def greet(devices):
    barrier = pltpu.get_barrier_semaphore()
    for device in devices:
        pl.semaphore_signal(barrier, inc=1, device_id=device, device_id_type=MESH)
    pl.semaphore_wait(barrier, len(devices))


class Sends:
    def __init__(self, send_sem, recv_sem):
        self.send_sem, self.recv_sem, self.started = send_sem, recv_sem, []

    def start(self, k, src, dst, device):
        copy = pltpu.make_async_remote_copy(
            src_ref=src,
            dst_ref=dst,
            send_sem=self.send_sem.at[k],
            recv_sem=self.recv_sem.at[k],
            device_id=device,
            device_id_type=MESH,
        )
        copy.start()
        self.started.append(copy)

    def arrived(self, k, dst):
        pltpu.make_async_copy(dst, dst, self.recv_sem.at[k]).wait()

    def drain(self):
        for copy in self.started:
            copy.wait_send()


def hx_gather_kernel(rows, cols, split, a, out, held, local_sem, send_sem, recv_sem):
    z_hi, x, core, y, z_lo = place()
    ctx = ctx_of(z_hi, x, core)
    right, left, far = (y + 1) % 4, (y + 3) % 4, (y + 2) % 4
    other = 1 - z_lo
    to_right, to_left, to_z = (ctx, right * 2 + z_lo), (ctx, left * 2 + z_lo), (ctx, y * 2 + other)
    load = pltpu.make_async_copy(a, held, local_sem.at[0])
    load.start()
    greet((to_right, to_left, to_z))

    first = (0, split)
    first_0, first_1 = (0, split // 2), (split // 2, split // 2)
    rest = (split, rows - split)
    half = (rows - split) // 2
    rest_0, rest_1 = (split, half), (split + half, half)

    def at(y_of, z_of, part):
        return out.at[pl.ds(part[0], part[1]), pl.ds((y_of * 2 + z_of) * cols, cols)]

    def own(part):
        return a.at[pl.ds(part[0], part[1]), :]

    sends = Sends(send_sem, recv_sem)

    def forward(k, y_of, z_of, part, device):
        sends.start(k, at(y_of, z_of, part), at(y_of, z_of, part), device)

    sends.start(0, own(first), at(y, z_lo, first), to_z)
    sends.start(1, own(first), at(y, z_lo, first), to_right)
    sends.start(2, own(first), at(y, z_lo, first), to_left)
    sends.start(3, own(rest), at(y, z_lo, rest), to_right)
    sends.start(4, own(rest), at(y, z_lo, rest), to_left)
    sends.start(5, own(rest), at(y, z_lo, rest), to_z)
    load.wait()
    keep = pltpu.make_async_copy(held, out.at[:, pl.ds((y * 2 + z_lo) * cols, cols)], local_sem.at[1])
    keep.start()
    sends.arrived(0, at(y, other, first))
    forward(6, y, other, first, to_right)
    forward(7, y, other, first, to_left)
    sends.arrived(3, at(left, z_lo, rest))
    forward(10, left, z_lo, rest_0, to_right)
    forward(11, left, z_lo, rest, to_z)
    sends.arrived(4, at(right, z_lo, rest))
    forward(12, right, z_lo, rest_1, to_left)
    forward(13, right, z_lo, rest, to_z)
    sends.arrived(1, at(left, z_lo, first))
    forward(8, left, z_lo, first_0, to_right)
    sends.arrived(2, at(right, z_lo, first))
    forward(9, right, z_lo, first_1, to_left)
    sends.arrived(6, at(left, other, first))
    forward(14, left, other, first_0, to_right)
    sends.arrived(7, at(right, other, first))
    forward(15, right, other, first_1, to_left)
    sends.arrived(10, at(far, z_lo, rest_0))
    forward(16, far, z_lo, rest_0, to_z)
    sends.arrived(12, at(far, z_lo, rest_1))
    forward(17, far, z_lo, rest_1, to_z)
    sends.arrived(5, at(y, other, rest))
    sends.arrived(8, at(far, z_lo, first_0))
    sends.arrived(9, at(far, z_lo, first_1))
    sends.arrived(11, at(left, other, rest))
    sends.arrived(13, at(right, other, rest))
    sends.arrived(14, at(far, other, first_0))
    sends.arrived(15, at(far, other, first_1))
    sends.arrived(16, at(far, other, rest_0))
    sends.arrived(17, at(far, other, rest_1))
    sends.drain()
    keep.wait()


def hx_gather(a, call_id, name):
    rows, cols = a.shape
    split = rows * 5 // 9 // 32 * 32
    sent = rows * cols * 2 * 7
    return pl.pallas_call(
        functools.partial(hx_gather_kernel, rows, cols, split),
        out_shape=jax.ShapeDtypeStruct((rows, cols * 8), a.dtype),
        in_specs=[pl.BlockSpec(memory_space=pl.ANY)],
        out_specs=pl.BlockSpec(memory_space=pl.ANY),
        scratch_shapes=[
            pltpu.VMEM((rows, cols), a.dtype),
            pltpu.SemaphoreType.DMA((2,)),
            pltpu.SemaphoreType.DMA((18,)),
            pltpu.SemaphoreType.DMA((18,)),
        ],
        compiler_params=pltpu.CompilerParams(collective_id=call_id, has_side_effects=True),
        name=name,
    )(a)


def ctx_gather_kernel(rows, a, out, transit, held, local_sem, send_sem, recv_sem):
    z_hi, x, core, y, z_lo = place()
    hx = y * 2 + z_lo
    z = z_hi * 2 + z_lo
    up, down = (z + 1) % 4, (z + 3) % 4
    right, left, far = (x + 1) % 4, (x + 3) % 4, (x + 2) % 4
    other = 1 - z_hi
    to_right, to_left = (ctx_of(z_hi, right, core), hx), (ctx_of(z_hi, left, core), hx)
    to_up = (ctx_of(up // 2, x, core), y * 2 + up % 2)
    to_down = (ctx_of(down // 2, x, core), y * 2 + down % 2)
    to_core = (ctx_of(z_hi, x, 1 - core), hx)
    load = pltpu.make_async_copy(a, held, local_sem.at[0])
    load.start()
    greet((to_right, to_left, to_up, to_down, to_core))
    whole, half_0, half_1 = (0, rows), (0, rows // 2), (rows // 2, rows // 2)

    def at(z_of, x_of, core_of, part):
        return out.at[pl.ds(ctx_of(z_of, x_of, core_of) * rows + part[0], part[1]), :]

    def own(part):
        return a.at[pl.ds(part[0], part[1]), :]

    sends = Sends(send_sem, recv_sem)

    def forward(k, z_of, x_of, part, device):
        sends.start(k, at(z_of, x_of, core, part), at(z_of, x_of, core, part), device)

    def arrived(k, z_of, x_of, part):
        sends.arrived(k, at(z_of, x_of, core, part))

    sends.start(0, own(half_0), transit.at[0], to_up)
    sends.start(1, own(half_1), transit.at[1], to_down)
    sends.start(2, own(whole), at(z_hi, x, core, whole), to_right)
    sends.start(3, own(whole), at(z_hi, x, core, whole), to_left)
    sends.start(4, own(whole), at(z_hi, x, core, whole), to_core)
    load.wait()
    keep = pltpu.make_async_copy(held, at(z_hi, x, core, whole), local_sem.at[1])
    keep.start()
    sends.arrived(0, transit.at[0])
    sends.start(5, transit.at[0], at(down // 2, x, core, half_0), to_up)
    sends.arrived(1, transit.at[1])
    sends.start(6, transit.at[1], at(up // 2, x, core, half_1), to_down)
    arrived(2, z_hi, left, whole)
    forward(10, z_hi, left, half_0, to_right)
    forward(11, z_hi, left, whole, to_core)
    arrived(3, z_hi, right, whole)
    forward(12, z_hi, right, half_1, to_left)
    forward(13, z_hi, right, whole, to_core)
    arrived(5, other, x, half_0)
    arrived(6, other, x, half_1)
    forward(7, other, x, whole, to_right)
    forward(8, other, x, whole, to_left)
    forward(9, other, x, whole, to_core)
    arrived(10, z_hi, far, half_0)
    arrived(12, z_hi, far, half_1)
    forward(18, z_hi, far, whole, to_core)
    arrived(7, other, left, whole)
    forward(14, other, left, half_0, to_right)
    forward(15, other, left, whole, to_core)
    arrived(8, other, right, whole)
    forward(16, other, right, half_1, to_left)
    forward(17, other, right, whole, to_core)
    arrived(14, other, far, half_0)
    arrived(16, other, far, half_1)
    forward(19, other, far, whole, to_core)

    def from_core(k, z_of, x_of):
        sends.arrived(k, at(z_of, x_of, 1 - core, whole))

    from_core(4, z_hi, x)
    from_core(11, z_hi, left)
    from_core(13, z_hi, right)
    from_core(9, other, x)
    from_core(18, z_hi, far)
    from_core(15, other, left)
    from_core(17, other, right)
    from_core(19, other, far)
    sends.drain()
    keep.wait()


def ctx_gather(a, call_id, name):
    rows, cols = a.shape
    return pl.pallas_call(
        functools.partial(ctx_gather_kernel, rows),
        out_shape=(
            jax.ShapeDtypeStruct((rows * 16, cols), a.dtype),
            jax.ShapeDtypeStruct((2, rows // 2, cols), a.dtype),
        ),
        in_specs=[pl.BlockSpec(memory_space=pl.ANY)],
        out_specs=(pl.BlockSpec(memory_space=pl.ANY), pl.BlockSpec(memory_space=pl.ANY)),
        scratch_shapes=[
            pltpu.VMEM((rows, cols), a.dtype),
            pltpu.SemaphoreType.DMA((2,)),
            pltpu.SemaphoreType.DMA((20,)),
            pltpu.SemaphoreType.DMA((20,)),
        ],
        compiler_params=pltpu.CompilerParams(collective_id=call_id, has_side_effects=True),
        name=name,
    )(a)[0]


def hx_spread_kernel(rows, cols, pick, a, out, held, local_sem, send_sem, recv_sem):
    ctx, me = lax.axis_index("ctx"), lax.axis_index("hx")

    def block(p):
        return a.at[:, pl.ds(p * cols, cols)] if pick else a

    load = pltpu.make_async_copy(block(me), held, local_sem.at[0])
    load.start()
    greet([(ctx, (me + k) % 8) for k in range(1, 8)])
    sends = Sends(send_sem, recv_sem)
    for k in range(1, 8):
        peer = (me + k) % 8
        sends.start(k, block(peer), out.at[pl.ds(me * rows, rows), :], (ctx, peer))
    load.wait()
    keep = pltpu.make_async_copy(held, out.at[pl.ds(me * rows, rows), :], local_sem.at[1])
    keep.start()
    for k in range(1, 8):
        sends.arrived(k, out.at[pl.ds((me + 8 - k) % 8 * rows, rows), :])
    sends.drain()
    keep.wait()


def hx_spread(a, cols, pick, call_id, name):
    rows = a.shape[0]
    return pl.pallas_call(
        functools.partial(hx_spread_kernel, rows, cols, pick),
        out_shape=jax.ShapeDtypeStruct((rows * 8, cols), a.dtype),
        in_specs=[pl.BlockSpec(memory_space=pl.ANY)],
        out_specs=pl.BlockSpec(memory_space=pl.ANY),
        scratch_shapes=[
            pltpu.VMEM((rows, cols), a.dtype),
            pltpu.SemaphoreType.DMA((2,)),
            pltpu.SemaphoreType.DMA((8,)),
            pltpu.SemaphoreType.DMA((8,)),
        ],
        compiler_params=pltpu.CompilerParams(collective_id=call_id, has_side_effects=True),
        name=name,
    )(a)


def ctx_exchange_kernel(rows, a, out, held, local_sem, send_sem, recv_sem):
    me, hx = lax.axis_index("ctx"), lax.axis_index("hx")

    def block(ref, p):
        return ref.at[pl.ds(p * rows, rows), :]

    load = pltpu.make_async_copy(block(a, me), held, local_sem.at[0])
    load.start()
    greet([((me + k) % 16, hx) for k in range(1, 16)])
    sends = Sends(send_sem, recv_sem)
    for k in range(1, 16):
        peer = (me + k) % 16
        sends.start(k, block(a, peer), block(out, me), (peer, hx))
    load.wait()
    keep = pltpu.make_async_copy(held, block(out, me), local_sem.at[1])
    keep.start()
    for k in range(1, 16):
        sends.arrived(k, block(out, (me + 16 - k) % 16))
    sends.drain()
    keep.wait()


def ctx_exchange(a, call_id, name):
    rows, cols = a.shape[0] // 16, a.shape[1]
    return pl.pallas_call(
        functools.partial(ctx_exchange_kernel, rows),
        out_shape=jax.ShapeDtypeStruct(a.shape, a.dtype),
        in_specs=[pl.BlockSpec(memory_space=pl.ANY)],
        out_specs=pl.BlockSpec(memory_space=pl.ANY),
        scratch_shapes=[
            pltpu.VMEM((rows, cols), a.dtype),
            pltpu.SemaphoreType.DMA((2,)),
            pltpu.SemaphoreType.DMA((16,)),
            pltpu.SemaphoreType.DMA((16,)),
        ],
        compiler_params=pltpu.CompilerParams(collective_id=call_id, has_side_effects=True),
        name=name,
    )(a)


def attend_kernel(q_t, kv, out):
    me = lax.axis_index("ctx")
    tok = q_t.shape[1]
    heads = q_t.shape[0] // HD
    scale = HD ** (-0.5) * math.log2(math.e)

    def visit(block, held, diagonal):
        at = pl.multiple_of(block * tok, tok)
        keys = kv[pl.ds(at, tok), :HD]
        values = kv[pl.ds(at, tok), HD:]
        new = []
        for h in range(heads):
            top, total, acc = held[h]
            scores = jnp.dot(keys, q_t[h * HD : (h + 1) * HD, :], preferred_element_type=jnp.float32) * scale
            if diagonal:
                key_pos = lax.broadcasted_iota(jnp.int32, scores.shape, 0)
                query_pos = lax.broadcasted_iota(jnp.int32, scores.shape, 1)
                scores = jnp.where(key_pos <= query_pos, scores, -1e30)
            new_top = jnp.maximum(top, jnp.max(scores, axis=0, keepdims=True))
            weights = jnp.exp2(scores - new_top)
            factor = jnp.exp2(top - new_top)
            total = total * factor + jnp.sum(weights, axis=0, keepdims=True)
            mixed = lax.dot_general(
                values,
                weights.astype(jnp.bfloat16),
                (((0,), (0,)), ((), ())),
                preferred_element_type=jnp.float32,
            )
            new.append((new_top, total, acc * factor + mixed))
        return tuple(new)

    start = tuple(
        (
            jnp.full((1, tok), -1e30, jnp.float32),
            jnp.zeros((1, tok), jnp.float32),
            jnp.zeros((HD, tok), jnp.float32),
        )
        for _ in range(heads)
    )
    held = visit(me, start, True)
    held = lax.fori_loop(0, me, lambda b, held: visit(b, held, False), held)
    for h in range(heads):
        top, total, acc = held[h]
        out[:, h * HD : (h + 1) * HD] = (acc / total).T.astype(out.dtype)


def attend(q_t, kv):
    cols, tok = q_t.shape
    return pl.pallas_call(
        attend_kernel,
        out_shape=jax.ShapeDtypeStruct((tok, cols), jnp.bfloat16),
        in_specs=[pl.BlockSpec(memory_space=pltpu.VMEM)] * 2,
        out_specs=pl.BlockSpec(memory_space=pltpu.VMEM),
        compiler_params=pltpu.CompilerParams(vmem_limit_bytes=48 << 20),
        cost_estimate=pl.CostEstimate(
            flops=cols * kv.shape[0] * tok * 4,
            bytes_accessed=kv.size * 2,
            transcendentals=cols // HD * tok * kv.shape[0],
        ),
        name="attend",
    )(q_t, kv)


def body(tokens, attn_gain, ffn_gain, w_query, w_key, w_value, w_out, w_router, routes, w_gate, w_up, w_down):
    f32, bf16 = jnp.float32, jnp.bfloat16
    hx = lax.axis_index("hx")
    tok_rows, full_width = tokens.shape
    width = full_width // 8
    q_cols = w_query.shape[1]

    out_cols = lax.all_to_all(w_out, "hx", split_axis=1, concat_axis=0, tiled=True)
    down_cols = lax.all_to_all(w_down[0], "hx", split_axis=1, concat_axis=0, tiled=True)

    weights = ctx_gather(jnp.concatenate((w_query, w_key, w_value), axis=1), 2, "gather_weights")
    floats = tokens.astype(f32)
    inverse = lax.rsqrt(jnp.mean(floats * floats, axis=-1, keepdims=True) + epsilon)
    normed = (floats * inverse * attn_gain.astype(f32)).astype(bf16)
    q_t = jnp.einsum("td,dc->ct", normed, weights[:, :q_cols], preferred_element_type=f32).astype(bf16)
    kv_own = jnp.dot(normed, weights[:, q_cols:], preferred_element_type=f32).astype(bf16)
    kv = ctx_gather(kv_own, 3, "gather_kv")
    attended = hx_gather(attend(q_t, kv), 4, "gather_attended")

    share = jnp.dot(attended, out_cols, preferred_element_type=f32)
    own_tokens = lax.dynamic_slice_in_dim(tokens, hx * width, width, 1)
    own_gain = lax.dynamic_slice_in_dim(ffn_gain, hx * width, width, 0).astype(f32)
    own_router = lax.dynamic_slice_in_dim(w_router, hx * width, width, 0)
    stream = (own_tokens.astype(f32) + share).astype(bf16)
    stream_f = stream.astype(f32)

    experts = w_router.shape[1]
    chosen = routes[:, 0]
    onehot = chosen[:, None] == jnp.arange(experts, dtype=jnp.int32)[None, :]
    capacity = tok_rows // 8
    counts = jnp.cumsum(onehot.astype(jnp.int32), axis=0)
    position = jnp.sum(jnp.where(onehot, counts, 0), axis=-1) - 1
    slot = chosen * capacity + position
    picks = (slot[None, :] == jnp.arange(experts * capacity, dtype=jnp.int32)[:, None]).astype(bf16)

    gained = stream_f * own_gain
    part_logits = jnp.dot(gained.astype(bf16), own_router, preferred_element_type=f32)
    part_logit = jnp.sum(jnp.where(onehot, part_logits, 0.0), axis=-1)
    part_square = jnp.sum(stream_f * stream_f, axis=-1)
    parts = jnp.concatenate(
        (part_square[None, :], part_logit[None, :], jnp.zeros((6, tok_rows), f32)), axis=0
    )
    sums = jnp.sum(hx_spread(parts, tok_rows, False, 7, "gather_sums").reshape(8, 8, tok_rows), axis=0)
    inverse2 = lax.rsqrt(sums[0] / full_width + epsilon)[:, None]
    score = jax.nn.sigmoid(sums[1][:, None] * inverse2)
    normed2 = (stream_f * inverse2 * own_gain).astype(bf16)
    routed = (normed2.astype(f32) * score).astype(bf16)
    buffer = jnp.dot(picks, routed, preferred_element_type=f32).astype(bf16)
    arrived = ctx_exchange(buffer, 6, "dispatch")
    rows = hx_gather(arrived, 1, "gather_rows")
    gate = jnp.dot(rows, w_gate[0], preferred_element_type=f32)
    up = jnp.dot(rows, w_up[0], preferred_element_type=f32)
    hidden = (jax.nn.silu(gate) * up).astype(bf16)
    hidden_all = hx_gather(hidden, 8, "gather_hidden")
    expert_rows = jnp.dot(hidden_all, down_cols, preferred_element_type=f32).astype(bf16)
    returned = ctx_exchange(expert_rows, 9, "give_back")
    expert_out = lax.dot_general(picks, returned, (((0,), (0,)), ((), ())), preferred_element_type=f32)
    return (stream_f + expert_out.astype(bf16).astype(f32)).astype(bf16)


def solution(mesh):
    in_specs = (
        P("ctx", None),
        P(),
        P(),
        P("ctx", "hx"),
        P("ctx", "hx"),
        P("ctx", "hx"),
        P("hx", None),
        P(),
        P("ctx", None),
        P("ctx", None, "hx"),
        P("ctx", None, "hx"),
        P("ctx", "hx", None),
    )
    return jax.shard_map(body, mesh=mesh, in_specs=in_specs, out_specs=P("ctx", "hx"), check_vma=False)
```

time: 906 us -> 494 us (0.55)
  waiting for transfers between devices: 696 us -> 0.01 us
  Pallas kernels: 0 us -> 391 us
  matrix products: 83 us -> 52.2 us
  blocking collectives: 27.2 us -> 0 us
  other arithmetic: 34.8 us -> 8.05 us
  between operations: 13.8 us -> 0.34 us
  local copies, waits for them, and re-layouts: 40.8 us -> 30.3 us
    all_gather x4 -> x0, waiting for transfers between devices: 429 us -> none  [the longest x1 204 us: body(): joined = lax.all_gather(arrived, HX, axis=3, tiled=True)]
    pallas_call x0 -> x9, Pallas kernels: none -> 391 us  [the longest x3 158 us: hx_gather(): pl.pallas_call(functools.partial(hx_gather_kernel, rows, cols, split), ou...]
    unnamed x9 -> x0, waiting for transfers between devices: 148 us -> none
    reduce_scatter x1 -> x0, waiting for transfers between devices: 98.7 us -> none  [summed_rows(): nearer = lax.psum_scatter(x, axes[0], scatter_dimension=dim, tiled=True)]
    dot_general x24 -> x9, matrix products: 83 us -> 52.2 us  [the longest x1 11.7 us: body(): jnp.dot(hidden_all, down_cols, preferred_element_type=f32).astype(bf16)]
    all_to_all x1 -> x0, blocking collectives: 27.2 us -> none  [body(): lax.all_to_all(buffer, 'ctx', split_axis=0, concat_axis=0, tiled=True)]
    all_to_all x1 -> x2, waiting for transfers between devices: 20.1 us -> 0.01 us  [the longest x1 0.01 us: body(): lax.all_to_all(w_down[0], 'hx', split_axis=1, concat_axis=0, tiled=True)]
    unnamed x25 -> x34, local copies, waits for them, and re-layouts: 34.6 us -> 15.7 us
  transfers between devices with their start and end apart: 8 -> 2, of which waited for: 8 -> 0; matrix products, arithmetic and copies ran while one was open for 1% -> 12% of each run, Pallas kernels for 0% -> 74%
where the time goes in v1:
time: 494 us; the launch traced here: 493 us
  Pallas kernels  391 us (79%)
  matrix products  52.2 us (11%)
  local copies, waits for them, and re-layouts  30.3 us (6%)
  starting transfers between devices  11.4 us (2%)
  other arithmetic  8.05 us (2%)
    pallas_call x3, Pallas kernels, hx_gather(): pl.pallas_call(functools.partial(hx_gather_kernel, rows, cols, split), ou...  158 us
    pallas_call x2, Pallas kernels, ctx_gather(): pl.pallas_call(functools.partial(ctx_gather_kernel, rows), out_shape=(jax...  92.1 us
    pallas_call x2, Pallas kernels, ctx_exchange(): pl.pallas_call(functools.partial(ctx_exchange_kernel, rows), out_shape=ja...  74.7 us
    pallas_call x1, Pallas kernels, hx_spread(): pl.pallas_call(functools.partial(hx_spread_kernel, rows, cols, pick), out...  62.2 us
    unnamed x34, local copies, waits for them, and re-layouts  15.7 us
    dot_general x1, matrix products, body(): jnp.dot(hidden_all, down_cols, preferred_element_type=f32).astype(bf16)  11.7 us
    dot_general x1, matrix products, body(): up = jnp.dot(rows, w_up[0], preferred_element_type=f32)  9.95 us
  transfers between devices with their start and end apart: 2, of which 0 were waited for; matrix products, arithmetic and copies ran while one was open for 12% of the time, Pallas kernels for 74%

profile of v1, /device:TPU:1, one launch (start us, length us, event | category | flops | bytes accessed | tf_op | source)
XLA Modules:
  0.0 492.9 jit_solution(9212898467977075456)
XLA Ops:
  0.0 6.3 %copy.15 = bf16[384,5120]{0,1:T(8,128)(2,1)} copy(bf16[384,5120]{1,0:T(8,128)(2,1)} %param.18) | data formatting | bytes 7864320 | tf_op args[6]
  6.4 6.5 %all-to-all-start = ((bf16[384,8,640]{0,2,1:T(8,128)(2,1)}), bf16[384,8,640]{0,2,1:T(8,128)(2,1)}, u32[]{:S(2)}, u32[]{:S(2)}) async-start(bf16[384,8,640]{0,2,1:T(8,128)(2,1)} %bitcast.45), calls=%async_computation | async-start | bytes 7864320 | tf_op jit(solution)/shard_map/all_to_all | solution.py:399
  12.9 1.2 reduce-window.6
  14.3 8.0 %copy.18 = bf16[1,512,5120]{1,2,0:T(8,128)(2,1)} copy(bf16[1,512,5120]{2,1,0:T(8,128)(2,1)} %param.23) | data formatting | bytes 10485760 | tf_op args[11]
  22.4 0.8 pad_maximum_fusion.a
  23.2 65.6 %gather_weights.1 = (bf16[5120,640]{1,0:T(8,128)(2,1)}, bf16[2,160,640]{2,1,0:T(8,128)(2,1)}) custom-call(bf16[320,640]{1,0:T(8,128)(2,1)} %pad_maximum_fusion.a), custom_call_target="tpu_custom_call" | custom-call | tf_op jit(solution)/shard_map/gather_weights/pallas_call | solution.py:230
  88.8 3.6 fusion
  92.4 5.6 %fusion.31.a = bf16[512,256]{1,0:T(8,128)(2,1)} fusion(bf16[5120,640]{1,0:T(8,128)(2,1)} %get-tuple-element.7, bf16[512,5120]{1,0:T(8,128)(2,1)} %param.12, f32[5120]{0:T(1024)S(1)} %convert_element_type.65, f32[512]{0:T(512)S(1)} %add_rsqrt_fusion), kind=kOutput, calls=%fused_computation.34 | convolution fusion | flops 1352794112 | bytes 8148992 | tf_op jit(solution)/shard_map/dot_general | solution.py:407
  98.0 26.5 %gather_kv.1 = (bf16[8192,256]{1,0:T(8,128)(2,1)}, bf16[2,256,256]{2,1,0:T(8,128)(2,1)}) custom-call(bf16[512,256]{1,0:T(8,128)(2,1)} %fusion.31.a), custom_call_target="tpu_custom_call" | custom-call | tf_op jit(solution)/shard_map/gather_kv/pallas_call | solution.py:230
  124.5 6.1 %fusion.26.q_t = bf16[384,512]{1,0:T(8,128)(2,1)S(1)} fusion(bf16[512,5120]{1,0:T(8,128)(2,1)} %param.12, f32[5120]{0:T(1024)S(1)} %convert_element_type.65, f32[512]{0:T(512)S(1)} %add_rsqrt_fusion, bf16[5120,640]{1,0:T(8,128)(2,1)} %get-tuple-element.7), kind=kOutput, calls=%fused_computation.33 | convolution fusion | flops 2023948288 | bytes 9590784 | tf_op jit(solution)/shard_map/td,dc->ct/dot_general | solution.py:406
  130.7 3.4 attend.1.a
  134.1 0.7 copy-done.2
  134.8 27.7 %gather_attended.1 = bf16[512,3072]{1,0:T(8,128)(2,1)} custom-call(bf16[512,384]{1,0:T(8,128)(2,1)} %copy-done.2), custom_call_target="tpu_custom_call" | custom-call | tf_op jit(solution)/shard_map/gather_attended/pallas_call | solution.py:131
  162.6 0.8 dynamic-slice_convert_fusion
  163.5 4.9 all-to-all-start.1
  168.4 6.5 %copy.16 = bf16[8,384,640]{2,1,0:T(8,128)(2,1)} copy(bf16[8,384,640]{1,2,0:T(8,128)(2,1)} %bitcast.1) | data formatting | bytes 7864320 | tf_op jit(solution)/shard_map/all_to_all | solution.py:399
  174.9 5.0 %fusion.22 = (f32[512]{0:T(512)S(1)}, bf16[512,640]{1,0:T(8,128)(2,1)S(1)}) fusion(bf16[512,3072]{1,0:T(8,128)(2,1)S(1)} %copy-done.5, bf16[3072,640]{1,0:T(8,128)(2,1)} %bitcast.47, bf16[512,5120]{1,0:T(8,128)(2,1)} %param.12, s32[]{:T(128)S(6)} %select_n.13), kind=kOutput, calls=%fused_computation.28 | convolution fusion | flops 2015231488 | bytes 8390660 | tf_op jit(solution)/shard_map/dot_general | solution.py:411
  179.8 0.3 fusion.36
  180.2 0.5 copy-done.12
  180.7 0.7 maximum_maximum_fusion.a
  181.3 62.2 %gather_sums.1 = f32[64,512]{1,0:T(8,128)} custom-call(f32[8,512]{1,0:T(8,128)} %maximum_maximum_fusion.a), custom_call_target="tpu_custom_call" | custom-call | tf_op jit(solution)/shard_map/gather_sums/pallas_call | solution.py:273
  243.6 0.9 bitcast_reduce_fusion
  244.5 3.4 fusion.15.a
  248.0 47.3 %dispatch.1.a = bf16[1024,640]{1,0:T(8,128)(2,1)} custom-call(bf16[1024,640]{1,0:T(8,128)(2,1)} %fusion.15.a), custom_call_target="tpu_custom_call" | custom-call | tf_op jit(solution)/shard_map/dispatch/pallas_call | solution.py:313
  295.3 73.4 %gather_rows.1 = bf16[1024,5120]{1,0:T(8,128)(2,1)} custom-call(bf16[1024,640]{1,0:T(8,128)(2,1)} %dispatch.1.a), custom_call_target="tpu_custom_call" | custom-call | tf_op jit(solution)/shard_map/gather_rows/pallas_call | solution.py:131
  368.8 9.9 %fusion.3 = f32[1024,512]{1,0:T(8,128)S(1)} fusion(bf16[1024,5120]{1,0:T(8,128)(2,1)} %gather_rows.1, bf16[1,5120,512]{2,1,0:T(8,128)(2,1)} %param.22), kind=kOutput, calls=%fused_computation.5 | convolution fusion | flops 5368709120 | bytes 17825792 | tf_op jit(solution)/shard_map/dot_general | solution.py:443
  378.8 6.9 %multiply_convert_fusion.a = bf16[1024,512]{1,0:T(8,128)(2,1)} fusion(f32[1024,512]{1,0:T(8,128)S(1)} %fusion.3, bf16[1024,5120]{1,0:T(8,128)(2,1)S(1)} %copy-done.4, bf16[1,5120,512]{2,1,0:T(8,128)(2,1)S(1)} %bitcast.58), kind=kOutput, calls=%fused_computation.17 | convolution fusion | flops 5371854848 | bytes 18874368 | tf_op jit(solution)/shard_map/dot_general | solution.py:442
  385.6 57.1 %gather_hidden.1 = bf16[1024,4096]{1,0:T(8,128)(2,1)} custom-call(bf16[1024,512]{1,0:T(8,128)(2,1)} %multiply_convert_fusion.a), custom_call_target="tpu_custom_call" | custom-call | tf_op jit(solution)/shard_map/gather_hidden/pallas_call | solution.py:131
  442.7 7.9 %copy.19 = bf16[8,512,640]{2,1,0:T(8,128)(2,1)} copy(bf16[8,512,640]{1,2,0:T(8,128)(2,1)} %bitcast.14) | data formatting | bytes 10485760 | tf_op jit(solution)/shard_map/all_to_all | solution.py:400
  450.6 11.7 %convolution_convert_fusion.a = bf16[1024,640]{1,0:T(8,128)(2,1)} fusion(bf16[1024,4096]{1,0:T(8,128)(2,1)} %gather_hidden.1, bf16[4096,640]{1,0:T(8,128)(2,1)} %bitcast.46), kind=kOutput, calls=%fused_computation.22 | convolution fusion | flops 5369364480 | bytes 14942208 | tf_op jit(solution)/shard_map/dot_general | solution.py:446
  462.3 27.4 %give_back.1 = bf16[1024,640]{1,0:T(8,128)(2,1)} custom-call(bf16[1024,640]{1,0:T(8,128)(2,1)} %convolution_convert_fusion.a), custom_call_target="tpu_custom_call" | custom-call | tf_op jit(solution)/shard_map/give_back/pallas_call | solution.py:313
  489.7 3.2 fusion.21
  (46 shorter events, 0.5 us)
Async XLA Ops:
  0.0 179.8 %copy-start = (bf16[5120,16]{0,1:T(8,128)(2,1)S(1)}, bf16[5120,16]{0,1:T(8,128)(2,1)}, u32[]{:S(2)}) copy-start(bf16[5120,16]{0,1:T(8,128)(2,1)} %param.19) | copy-start | bytes 491524
  6.3 6.5 %copy-start.9 = (s32[512,1]{0,1:T(1,128)S(1)}, s32[512,1]{0,1:T(1,128)}, u32[]{:S(2)}) copy-start(s32[512,1]{0,1:T(1,128)} %param.20) | copy-start | bytes 6148
  6.4 7.9 %copy-start.10 = (bf16[5120]{0:T(1024)(128)(2,1)S(1)}, bf16[5120]{0:T(1024)(128)(2,1)}, u32[]{:S(2)}) copy-start(bf16[5120]{0:T(1024)(128)(2,1)} %param.13) | copy-start | bytes 30724
  6.4 157.1 %all-to-all-start = ((bf16[384,8,640]{0,2,1:T(8,128)(2,1)}), bf16[384,8,640]{0,2,1:T(8,128)(2,1)}, u32[]{:S(2)}, u32[]{:S(2)}) async-start(bf16[384,8,640]{0,2,1:T(8,128)(2,1)} %bitcast.45), calls=%async_computation | async-start | bytes 7864320 | tf_op jit(solution)/shard_map/all_to_all | solution.py:399
  14.3 8.1 %copy-start.11 = (s32[16,5]{0,1:T(8,128)}, s32[16,5]{0,1:T(8,128)S(1)}, u32[]{:S(2)}) copy-start(s32[16,5]{0,1:T(8,128)S(1)} %reduce-window.9) | copy-start | bytes 964
  14.3 8.1 %copy-start.6 = (bf16[320,384]{1,0:T(8,128)(2,1)S(1)}, bf16[320,384]{1,0:T(8,128)(2,1)}, u32[]{:S(2)}) copy-start(bf16[320,384]{1,0:T(8,128)(2,1)} %param.15) | copy-start | bytes 737284
  14.3 8.1 %copy-start.7 = (bf16[320,128]{1,0:T(8,128)(2,1)S(1)}, bf16[320,128]{1,0:T(8,128)(2,1)}, u32[]{:S(2)}) copy-start(bf16[320,128]{1,0:T(8,128)(2,1)} %param.17) | copy-start | bytes 245764
  14.3 8.0 %copy-start.8 = (bf16[320,128]{1,0:T(8,128)(2,1)S(1)}, bf16[320,128]{1,0:T(8,128)(2,1)}, u32[]{:S(2)}) copy-start(bf16[320,128]{1,0:T(8,128)(2,1)} %param.16) | copy-start | bytes 245764
  124.5 6.2 %copy-start.3 = (bf16[8192,256]{1,0:T(8,128)(2,1)S(1)}, bf16[8192,256]{1,0:T(8,128)(2,1)}, u32[]{:S(2)}) copy-start(bf16[8192,256]{1,0:T(8,128)(2,1)} %get-tuple-element.8.kv) | copy-start | bytes 12582916
  130.7 32.7 %slice-start = ((s32[16,5]{0,1:T(8,128)}), s32[16,4]{0,1:T(4,128)S(1)}, s32[]{:S(2)}) async-start(s32[16,5]{0,1:T(8,128)} %copy-done.11), calls=%async_computation.2 | async-start | bytes 4096 | tf_op jit(solution)/shard_map/slice.1
  134.1 0.7 copy-start.2
  163.5 279.3 %all-to-all-start.1 = ((bf16[512,8,640]{0,2,1:T(8,128)(2,1)}), bf16[512,8,640]{0,2,1:T(8,128)(2,1)}, u32[]{:S(2)}, u32[]{:S(2)}) async-start(bf16[512,8,640]{0,2,1:T(8,128)(2,1)} %bitcast.44), calls=%async_computation.1 | async-start | bytes 10485760 | tf_op jit(solution)/shard_map/all_to_all | solution.py:400
  168.4 6.5 %copy-start.5 = (bf16[512,3072]{1,0:T(8,128)(2,1)S(1)}, bf16[512,3072]{1,0:T(8,128)(2,1)}, u32[]{:S(2)}) copy-start(bf16[512,3072]{1,0:T(8,128)(2,1)} %gather_attended.1) | copy-start | bytes 9437188
  179.8 0.8 copy-start.12
  295.3 83.4 %slice-start.1 = ((s8[5242880]{0:T(1024)(128)(4,1)}), s8[1048576]{0:T(1024)(128)(4,1)S(1)}, s32[]{:S(2)}) async-start(s8[5242880]{0:T(1024)(128)(4,1)} %bitcast.57), calls=%async_computation.3 | async-start | bytes 2097152
  368.7 10.0 %copy-start.4 = (bf16[1024,5120]{1,0:T(8,128)(2,1)S(1)}, bf16[1024,5120]{1,0:T(8,128)(2,1)}, u32[]{:S(2)}) copy-start(bf16[1024,5120]{1,0:T(8,128)(2,1)} %gather_rows.1) | copy-start | bytes 31457284
  368.8 10.0 %slice-start.2 = ((s8[5242880]{0:T(1024)(128)(4,1)}), s8[4194304]{0:T(1024)(128)(4,1)S(1)}, s32[]{:S(2)}) async-start(s8[5242880]{0:T(1024)(128)(4,1)} %bitcast.57), calls=%async_computation.4 | async-start | bytes 8388608
  450.6 39.1 %copy-start.13 = (bf16[512,640]{1,0:T(8,128)(2,1)S(1)}, bf16[512,640]{1,0:T(8,128)(2,1)}, u32[]{:S(2)}) copy-start(bf16[512,640]{1,0:T(8,128)(2,1)} %copy-done.12) | copy-start | bytes 1966084
  450.6 42.3 %copy-start.1 = (bf16[5120,16]{0,1:T(8,128)(2,1)S(1)}, bf16[5120,16]{0,1:T(8,128)(2,1)}, u32[]{:S(2)}) copy-start(bf16[5120,16]{0,1:T(8,128)(2,1)} %param.19) | copy-start | bytes 491524

commit v2 on v1

--- a/solution.py
+++ b/solution.py
@@ -144,7 +144,7 @@
     )(a)
 
 
-def ctx_gather_kernel(rows, a, out, transit, held, local_sem, send_sem, recv_sem):
+def ctx_gather_steps(rows, a, out, transit, sends, keep_own, hooks):
     z_hi, x, core, y, z_lo = place()
     hx = y * 2 + z_lo
     z = z_hi * 2 + z_lo
@@ -155,9 +155,6 @@
     to_up = (ctx_of(up // 2, x, core), y * 2 + up % 2)
     to_down = (ctx_of(down // 2, x, core), y * 2 + down % 2)
     to_core = (ctx_of(z_hi, x, 1 - core), hx)
-    load = pltpu.make_async_copy(a, held, local_sem.at[0])
-    load.start()
-    greet((to_right, to_left, to_up, to_down, to_core))
     whole, half_0, half_1 = (0, rows), (0, rows // 2), (rows // 2, rows // 2)
 
     def at(z_of, x_of, core_of, part):
@@ -165,8 +162,6 @@
 
     def own(part):
         return a.at[pl.ds(part[0], part[1]), :]
-
-    sends = Sends(send_sem, recv_sem)
 
     def forward(k, z_of, x_of, part, device):
         sends.start(k, at(z_of, x_of, core, part), at(z_of, x_of, core, part), device)
@@ -179,13 +174,12 @@
     sends.start(2, own(whole), at(z_hi, x, core, whole), to_right)
     sends.start(3, own(whole), at(z_hi, x, core, whole), to_left)
     sends.start(4, own(whole), at(z_hi, x, core, whole), to_core)
-    load.wait()
-    keep = pltpu.make_async_copy(held, at(z_hi, x, core, whole), local_sem.at[1])
-    keep.start()
+    keep_own(at(z_hi, x, core, whole))
     sends.arrived(0, transit.at[0])
     sends.start(5, transit.at[0], at(down // 2, x, core, half_0), to_up)
     sends.arrived(1, transit.at[1])
     sends.start(6, transit.at[1], at(up // 2, x, core, half_1), to_down)
+    hooks[0]()
     arrived(2, z_hi, left, whole)
     forward(10, z_hi, left, half_0, to_right)
     forward(11, z_hi, left, whole, to_core)
@@ -197,9 +191,11 @@
     forward(7, other, x, whole, to_right)
     forward(8, other, x, whole, to_left)
     forward(9, other, x, whole, to_core)
+    hooks[1]()
     arrived(10, z_hi, far, half_0)
     arrived(12, z_hi, far, half_1)
     forward(18, z_hi, far, whole, to_core)
+    hooks[2]()
     arrived(7, other, left, whole)
     forward(14, other, left, half_0, to_right)
     forward(15, other, left, whole, to_core)
@@ -221,29 +217,205 @@
     from_core(15, other, left)
     from_core(17, other, right)
     from_core(19, other, far)
+
+
+def ctx_neighbours():
+    z_hi, x, core, y, z_lo = place()
+    hx = y * 2 + z_lo
+    z = z_hi * 2 + z_lo
+    up, down = (z + 1) % 4, (z + 3) % 4
+    return (
+        (ctx_of(z_hi, (x + 1) % 4, core), hx),
+        (ctx_of(z_hi, (x + 3) % 4, core), hx),
+        (ctx_of(up // 2, x, core), y * 2 + up % 2),
+        (ctx_of(down // 2, x, core), y * 2 + down % 2),
+        (ctx_of(z_hi, x, 1 - core), hx),
+    )
+
+
+def gather_weights_kernel(
+    rows, a, w_out, w_down, out, transit, out_cols, down_cols, held, held_out, held_down, local_sem, send_sem, recv_sem
+):
+    z_hi, x, core, y, z_lo = place()
+    ctx, me = ctx_of(z_hi, x, core), y * 2 + z_lo
+    depth, width = w_out.shape[0], out_cols.shape[1]
+    deep = w_down.shape[0]
+    part = depth // 2
+    mine = pl.ds(me * width, width)
+    loads = (
+        pltpu.make_async_copy(a, held, local_sem.at[0]),
+        pltpu.make_async_copy(w_out.at[:, mine], held_out, local_sem.at[1]),
+        pltpu.make_async_copy(w_down.at[:, mine], held_down, local_sem.at[2]),
+    )
+    for load in loads:
+        load.start()
+    greet(ctx_neighbours() + tuple((ctx, (me + k) % 8) for k in range(1, 8)))
+    sends = Sends(send_sem, recv_sem)
+    keeps = []
+
+    def cut(y_step, flip):
+        return (y + y_step) % 4 * 2 + (1 - z_lo if flip else z_lo)
+
+    order = ((1, 0), (3, 0), (2, 0), (0, 1), (1, 1), (3, 1), (2, 1))
+
+    def share(i):
+        peer = cut(*order[i])
+        src = w_out.at[pl.ds(core * part, part), pl.ds(peer * width, width)]
+        sends.start(20 + i, src, out_cols.at[pl.ds(me * depth + core * part, part), :], (ctx, peer))
+
+    def keep_own(place_own):
+        for load in loads:
+            load.wait()
+        for held_ref, dst in (
+            (held, place_own),
+            (held_out, out_cols.at[pl.ds(me * depth, depth), :]),
+            (held_down, down_cols.at[pl.ds(me * deep, deep), :]),
+        ):
+            keep = pltpu.make_async_copy(held_ref, dst, local_sem.at[3 + len(keeps)])
+            keep.start()
+            keeps.append(keep)
+        for i in range(3):
+            share(i)
+
+    def cross():
+        for i in range(3, 7):
+            share(i)
+        peer = cut(0, 1)
+        src = w_down.at[pl.ds(0, deep // 2), pl.ds(peer * width, width)]
+        sends.start(34, src, down_cols.at[pl.ds(me * deep, deep // 2), :], (ctx, peer))
+
+    def hand_on(first, last):
+        for i in range(first, last):
+            y_step, flip = order[i]
+            source = cut((4 - y_step) % 4, flip)
+            block = out_cols.at[pl.ds(source * depth + core * part, part), :]
+            sends.arrived(20 + i, block)
+            sends.start(27 + i, block, block, (ctx_of(z_hi, x, 1 - core), me))
+
+    ctx_gather_steps(
+        rows, a, out, transit, sends, keep_own, (cross, lambda: hand_on(0, 2), lambda: hand_on(2, 3))
+    )
+    hand_on(3, 7)
+    for i in range(7):
+        y_step, flip = order[i]
+        source = cut((4 - y_step) % 4, flip)
+        sends.arrived(27 + i, out_cols.at[pl.ds(source * depth + (1 - core) * part, part), :])
+    sends.arrived(34, down_cols.at[pl.ds(cut(0, 1) * deep, deep // 2), :])
     sends.drain()
-    keep.wait()
-
-
-def ctx_gather(a, call_id, name):
+    for keep in keeps:
+        keep.wait()
+
+
+ANY = pl.BlockSpec(memory_space=pl.ANY)
+
+
+def gather_weights(a, w_out, w_down, call_id):
     rows, cols = a.shape
-    return pl.pallas_call(
-        functools.partial(ctx_gather_kernel, rows),
+    depth, deep, width = w_out.shape[0], w_down.shape[0], w_out.shape[1] // 8
+    weights, _, out_cols, down_cols = pl.pallas_call(
+        functools.partial(gather_weights_kernel, rows),
         out_shape=(
             jax.ShapeDtypeStruct((rows * 16, cols), a.dtype),
             jax.ShapeDtypeStruct((2, rows // 2, cols), a.dtype),
+            jax.ShapeDtypeStruct((depth * 8, width), a.dtype),
+            jax.ShapeDtypeStruct((deep * 8, width), a.dtype),
         ),
-        in_specs=[pl.BlockSpec(memory_space=pl.ANY)],
-        out_specs=(pl.BlockSpec(memory_space=pl.ANY), pl.BlockSpec(memory_space=pl.ANY)),
+        in_specs=[ANY] * 3,
+        out_specs=(ANY,) * 4,
+        scratch_shapes=[
+            pltpu.VMEM((rows, cols), a.dtype),
+            pltpu.VMEM((depth, width), a.dtype),
+            pltpu.VMEM((deep, width), a.dtype),
+            pltpu.SemaphoreType.DMA((6,)),
+            pltpu.SemaphoreType.DMA((35,)),
+            pltpu.SemaphoreType.DMA((35,)),
+        ],
+        compiler_params=pltpu.CompilerParams(collective_id=call_id, has_side_effects=True),
+        name="gather_weights",
+    )(a, w_out, w_down)
+    return weights, out_cols, down_cols
+
+
+def gather_kv_kernel(rows, a, w_down, _, out, transit, passing, down_cols, held, local_sem, send_sem, recv_sem):
+    z_hi, x, core, y, z_lo = place()
+    ctx, me = ctx_of(z_hi, x, core), y * 2 + z_lo
+    deep, width = w_down.shape[0], down_cols.shape[1]
+    half = deep // 2
+    right, left, far, other = (y + 1) % 4, (y + 3) % 4, (y + 2) % 4, 1 - z_lo
+    to_right, to_left = (ctx, right * 2 + z_lo), (ctx, left * 2 + z_lo)
+    across_right, across_left = (ctx, right * 2 + other), (ctx, left * 2 + other)
+    load = pltpu.make_async_copy(a, held, local_sem.at[0])
+    load.start()
+    greet(ctx_neighbours() + (to_right, to_left, across_right, across_left, (ctx, y * 2 + other)))
+    sends = Sends(send_sem, recv_sem)
+    keeps = []
+
+    def cut(h, target):
+        return w_down.at[pl.ds(h * half, half), pl.ds(target * width, width)]
+
+    def rows_of(source, h):
+        return down_cols.at[pl.ds(source * deep + h * half, half), :]
+
+    def keep_own(place_own):
+        load.wait()
+        keep = pltpu.make_async_copy(held, place_own, local_sem.at[1])
+        keep.start()
+        keeps.append(keep)
+        sends.start(20, cut(0, far * 2 + z_lo), passing.at[0], to_right)
+        sends.start(21, cut(0, far * 2 + other), passing.at[1], to_right)
+        sends.start(22, cut(1, far * 2 + z_lo), passing.at[2], to_left)
+        sends.start(23, cut(1, far * 2 + other), passing.at[3], to_left)
+
+    def cross():
+        sends.start(28, cut(1, y * 2 + other), rows_of(me, 1), (ctx, y * 2 + other))
+
+    def near():
+        sends.arrived(20, passing.at[0])
+        sends.start(24, passing.at[0], rows_of(left * 2 + z_lo, 0), to_right)
+        sends.arrived(22, passing.at[2])
+        sends.start(26, passing.at[2], rows_of(right * 2 + z_lo, 1), to_left)
+
+    def across():
+        sends.arrived(21, passing.at[1])
+        sends.start(25, passing.at[1], rows_of(left * 2 + z_lo, 0), across_right)
+        sends.arrived(23, passing.at[3])
+        sends.start(27, passing.at[3], rows_of(right * 2 + z_lo, 1), across_left)
+
+    ctx_gather_steps(rows, a, out, transit, sends, keep_own, (cross, near, across))
+    sends.arrived(28, rows_of(y * 2 + other, 1))
+    sends.arrived(24, rows_of(far * 2 + z_lo, 0))
+    sends.arrived(26, rows_of(far * 2 + z_lo, 1))
+    sends.arrived(25, rows_of(far * 2 + other, 0))
+    sends.arrived(27, rows_of(far * 2 + other, 1))
+    sends.drain()
+    for keep in keeps:
+        keep.wait()
+
+
+def gather_kv(a, w_down, down_cols, call_id):
+    rows, cols = a.shape
+    deep, width = w_down.shape[0], w_down.shape[1] // 8
+    kv, _, _, down_cols = pl.pallas_call(
+        functools.partial(gather_kv_kernel, rows),
+        out_shape=(
+            jax.ShapeDtypeStruct((rows * 16, cols), a.dtype),
+            jax.ShapeDtypeStruct((2, rows // 2, cols), a.dtype),
+            jax.ShapeDtypeStruct((4, deep // 2, width), a.dtype),
+            jax.ShapeDtypeStruct((deep * 8, width), a.dtype),
+        ),
+        in_specs=[ANY] * 3,
+        out_specs=(ANY,) * 4,
+        input_output_aliases={2: 3},
         scratch_shapes=[
             pltpu.VMEM((rows, cols), a.dtype),
             pltpu.SemaphoreType.DMA((2,)),
-            pltpu.SemaphoreType.DMA((20,)),
-            pltpu.SemaphoreType.DMA((20,)),
+            pltpu.SemaphoreType.DMA((29,)),
+            pltpu.SemaphoreType.DMA((29,)),
         ],
         compiler_params=pltpu.CompilerParams(collective_id=call_id, has_side_effects=True),
-        name=name,
-    )(a)[0]
+        name="gather_kv",
+    )(a, w_down, down_cols)
+    return kv, down_cols
 
 
 def hx_spread_kernel(rows, cols, pick, a, out, held, local_sem, send_sem, recv_sem):
@@ -326,8 +498,21 @@
     )(a)
 
 
-def attend_kernel(q_t, kv, out):
-    me = lax.axis_index("ctx")
+def attend_kernel(q_t, kv, w_down, _, out, down_cols, send_sem, recv_sem):
+    me, hx = lax.axis_index("ctx"), lax.axis_index("hx")
+    y, z_lo = hx // 2, hx % 2
+    deep, width = w_down.shape[0], down_cols.shape[1]
+    order = ((1, 0), (3, 1), (1, 1), (3, 0))
+
+    def peer_of(y_step, flip):
+        return (y + y_step) % 4 * 2 + (1 - z_lo if flip else z_lo)
+
+    greet([(me, peer_of(*step)) for step in order])
+    sends = Sends(send_sem, recv_sem)
+    for i, step in enumerate(order):
+        peer = peer_of(*step)
+        src = w_down.at[:, pl.ds(peer * width, width)]
+        sends.start(i, src, down_cols.at[pl.ds(hx * deep, deep), :], (me, peer))
     tok = q_t.shape[1]
     heads = q_t.shape[0] // HD
     scale = HD ** (-0.5) * math.log2(math.e)
@@ -370,23 +555,34 @@
     for h in range(heads):
         top, total, acc = held[h]
         out[:, h * HD : (h + 1) * HD] = (acc / total).T.astype(out.dtype)
-
-
-def attend(q_t, kv):
+    for i, (y_step, flip) in enumerate(order):
+        source = peer_of(4 - y_step, flip)
+        sends.arrived(i, down_cols.at[pl.ds(source * deep, deep), :])
+    sends.drain()
+
+
+def attend(q_t, kv, w_down, down_cols, call_id):
     cols, tok = q_t.shape
     return pl.pallas_call(
         attend_kernel,
-        out_shape=jax.ShapeDtypeStruct((tok, cols), jnp.bfloat16),
-        in_specs=[pl.BlockSpec(memory_space=pltpu.VMEM)] * 2,
-        out_specs=pl.BlockSpec(memory_space=pltpu.VMEM),
-        compiler_params=pltpu.CompilerParams(vmem_limit_bytes=48 << 20),
+        out_shape=(
+            jax.ShapeDtypeStruct((tok, cols), jnp.bfloat16),
+            jax.ShapeDtypeStruct(down_cols.shape, jnp.bfloat16),
+        ),
+        in_specs=[pl.BlockSpec(memory_space=pltpu.VMEM)] * 2 + [ANY] * 2,
+        out_specs=(pl.BlockSpec(memory_space=pltpu.VMEM), ANY),
+        input_output_aliases={3: 1},
+        scratch_shapes=[pltpu.SemaphoreType.DMA((4,)), pltpu.SemaphoreType.DMA((4,))],
+        compiler_params=pltpu.CompilerParams(
+            vmem_limit_bytes=48 << 20, collective_id=call_id, has_side_effects=True
+        ),
         cost_estimate=pl.CostEstimate(
             flops=cols * kv.shape[0] * tok * 4,
             bytes_accessed=kv.size * 2,
             transcendentals=cols // HD * tok * kv.shape[0],
         ),
         name="attend",
-    )(q_t, kv)
+    )(q_t, kv, w_down, down_cols)
 
 
 def body(tokens, attn_gain, ffn_gain, w_query, w_key, w_value, w_out, w_router, routes, w_gate, w_up, w_down):
@@ -396,17 +592,19 @@
     width = full_width // 8
     q_cols = w_query.shape[1]
 
-    out_cols = lax.all_to_all(w_out, "hx", split_axis=1, concat_axis=0, tiled=True)
-    down_cols = lax.all_to_all(w_down[0], "hx", split_axis=1, concat_axis=0, tiled=True)
-
-    weights = ctx_gather(jnp.concatenate((w_query, w_key, w_value), axis=1), 2, "gather_weights")
+    w_down = w_down[0]
+
+    weights, out_cols, down_cols = gather_weights(
+        jnp.concatenate((w_query, w_key, w_value), axis=1), w_out, w_down, 2
+    )
     floats = tokens.astype(f32)
     inverse = lax.rsqrt(jnp.mean(floats * floats, axis=-1, keepdims=True) + epsilon)
     normed = (floats * inverse * attn_gain.astype(f32)).astype(bf16)
     q_t = jnp.einsum("td,dc->ct", normed, weights[:, :q_cols], preferred_element_type=f32).astype(bf16)
     kv_own = jnp.dot(normed, weights[:, q_cols:], preferred_element_type=f32).astype(bf16)
-    kv = ctx_gather(kv_own, 3, "gather_kv")
-    attended = hx_gather(attend(q_t, kv), 4, "gather_attended")
+    kv, down_cols = gather_kv(kv_own, w_down, down_cols, 3)
+    attended, down_cols = attend(q_t, kv, w_down, down_cols, 5)
+    attended = hx_gather(attended, 4, "gather_attended")
 
     share = jnp.dot(attended, out_cols, preferred_element_type=f32)
     own_tokens = lax.dynamic_slice_in_dim(tokens, hx * width, width, 1)

time: 494 us -> 410 us (0.83)
  Pallas kernels: 391 us -> 341 us
  local copies, waits for them, and re-layouts: 30.3 us -> 3.25 us
  starting transfers between devices: 11.4 us -> 0 us
    pallas_call x1, Pallas kernels: 62.2 us -> 5.87 us  [hx_spread(): pl.pallas_call(functools.partial(hx_spread_kernel, rows, cols, pick), out...]
    pallas_call x3, Pallas kernels: 95.5 us -> 127 us  [the longest x1 57.9 us: gather_weights(): pl.pallas_call(functools.partial(gather_weights_kernel, rows), out_shape=...]
    pallas_call x2, Pallas kernels: 74.7 us -> 55.1 us  [ctx_exchange(): pl.pallas_call(functools.partial(ctx_exchange_kernel, rows), out_shape=ja...]
    all_to_all x2 -> x0, local copies, waits for them, and re-layouts: 14.3 us -> none  [the longest x1 7.85 us: body(): lax.all_to_all(w_down[0], 'hx', split_axis=1, concat_axis=0, tiled=True)]
    unnamed x34 -> x18, local copies, waits for them, and re-layouts: 15.7 us -> 2.95 us
    all_to_all x2 -> x0, starting transfers between devices: 11.4 us -> none  [the longest x1 6.49 us: body(): lax.all_to_all(w_out, 'hx', split_axis=1, concat_axis=0, tiled=True)]
    pallas_call x3, Pallas kernels: 158 us -> 153 us  [hx_gather(): pl.pallas_call(functools.partial(hx_gather_kernel, rows, cols, split), ou...]
  transfers between devices with their start and end apart: 2 -> 0, of which waited for: 0 -> 0; matrix products, arithmetic and copies ran while one was open for 12% -> 0% of each run, Pallas kernels for 74% -> 0%
where the time goes in v2:
time: 410 us; the launch traced here: 409 us
  Pallas kernels  341 us (83%)
  matrix products  53.5 us (13%)
  other arithmetic  10.9 us (3%)
    pallas_call x3, Pallas kernels, hx_gather(): pl.pallas_call(functools.partial(hx_gather_kernel, rows, cols, split), ou...  153 us
    pallas_call x1, Pallas kernels, gather_weights(): pl.pallas_call(functools.partial(gather_weights_kernel, rows), out_shape=...  57.9 us
    pallas_call x2, Pallas kernels, ctx_exchange(): pl.pallas_call(functools.partial(ctx_exchange_kernel, rows), out_shape=ja...  55.1 us
    pallas_call x1, Pallas kernels, gather_kv(): pl.pallas_call(functools.partial(gather_kv_kernel, rows), out_shape=(jax....  38.2 us
    pallas_call x1, Pallas kernels, attend(): pl.pallas_call(attend_kernel, out_shape=(jax.ShapeDtypeStruct((tok, cols)...  31.3 us
    dot_general x1, matrix products, body(): jnp.dot(hidden_all, down_cols, preferred_element_type=f32).astype(bf16)  11.5 us
    dot_general x1, matrix products, body(): up = jnp.dot(rows, w_up[0], preferred_element_type=f32)  10.2 us
    dot_general x1, matrix products, body(): gate = jnp.dot(rows, w_gate[0], preferred_element_type=f32)  8.52 us

profile of v2, /device:TPU:1, one launch (start us, length us, event | category | flops | bytes accessed | tf_op | source)
XLA Modules:
  0.0 409.1 jit_solution(6153205520096013380)
XLA Ops:
  0.0 0.7 fusion.47
  0.8 1.1 reduce-window.6
  1.9 0.2 slice_reduce_fusion
  2.2 0.8 fusion.46
  2.9 0.7 add_add_fusion
  3.6 0.7 convert_element_type.65
  4.3 3.6 fusion
  8.0 0.8 pad_maximum_fusion.a
  8.8 57.9 %gather_weights.1 = (bf16[5120,640]{1,0:T(8,128)(2,1)}, bf16[2,160,640]{2,1,0:T(8,128)(2,1)}, bf16[3072,640]{1,0:T(8,128)(2,1)}, bf16[4096,640]{1,0:T(8,128)(2,1)}) custom-call(bf16[320,640]{1,0:T(8,128)(2,1)} %pad_maximum_fusion.a, bf16[384,5120]{1,0:T(8,128)(2,1)} %w_out.1, bf16[512,5120]{1,0:T(8,128)(2,1)} %bitcast.39), custom_call_target="tpu_custom_call" | custom-call | tf_op jit(solution)/shard_map/gather_weights/pallas_call | solution.py:315
  66.6 6.0 %fusion.26.q_t = bf16[384,512]{1,0:T(8,128)(2,1)S(1)} fusion(bf16[512,5120]{1,0:T(8,128)(2,1)} %param.12, f32[5120]{0:T(1024)S(1)} %convert_element_type.65, f32[512]{0:T(512)S(1)} %add_rsqrt_fusion, bf16[5120,640]{1,0:T(8,128)(2,1)} %get-tuple-element.12), kind=kOutput, calls=%fused_computation.33 | convolution fusion | flops 2023948288 | bytes 9590784 | tf_op jit(solution)/shard_map/td,dc->ct/dot_general | solution.py:603
  72.7 5.6 %fusion.31.a = bf16[512,256]{1,0:T(8,128)(2,1)} fusion(bf16[5120,640]{1,0:T(8,128)(2,1)} %get-tuple-element.12, bf16[512,5120]{1,0:T(8,128)(2,1)} %param.12, f32[5120]{0:T(1024)S(1)} %convert_element_type.65, f32[512]{0:T(512)S(1)} %add_rsqrt_fusion), kind=kOutput, calls=%fused_computation.34 | convolution fusion | flops 1352794112 | bytes 8148992 | tf_op jit(solution)/shard_map/dot_general | solution.py:604
  78.2 38.2 %gather_kv.1 = (bf16[8192,256]{1,0:T(8,128)(2,1)}, bf16[2,256,256]{2,1,0:T(8,128)(2,1)}, bf16[4,256,640]{2,1,0:T(8,128)(2,1)}, bf16[4096,640]{1,0:T(8,128)(2,1)}) custom-call(bf16[512,256]{1,0:T(8,128)(2,1)} %fusion.31.a, bf16[512,5120]{1,0:T(8,128)(2,1)} %bitcast.40, bf16[4096,640]{1,0:T(8,128)(2,1)} %get-tuple-element.13._), custom_call_target="tpu_custom_call", output_to_operand_aliasing={{3}: (2, {})} | custom-call | tf_op jit(solution)/shard_map/gather_kv/pallas_call | solution.py:398
  116.4 2.2 copy-done.3
  118.6 31.3 %attend.1 = (bf16[512,384]{1,0:T(8,128)(2,1)S(1)}, bf16[4096,640]{1,0:T(8,128)(2,1)}) custom-call(bf16[384,512]{1,0:T(8,128)(2,1)S(1)} %fusion.26.q_t, bf16[8192,256]{1,0:T(8,128)(2,1)S(1)} %copy-done.3, bf16[512,5120]{1,0:T(8,128)(2,1)} %bitcast.41, bf16[4096,640]{1,0:T(8,128)(2,1)} %get-tuple-element.15._), custom_call_target="tpu_custom_call", output_to_operand_aliasing={{1}: (3, {})} | custom-call | flops 6442450944 | bytes 4194304 | tf_op jit(solution)/shard_map/attend/pallas_call | solution.py:566
  149.9 0.7 copy-done.2
  150.6 22.4 %gather_attended.1 = bf16[512,3072]{1,0:T(8,128)(2,1)} custom-call(bf16[512,384]{1,0:T(8,128)(2,1)} %copy-done.2), custom_call_target="tpu_custom_call" | custom-call | tf_op jit(solution)/shard_map/gather_attended/pallas_call | solution.py:131
  173.1 5.9 %fusion.22 = (f32[512]{0:T(512)S(1)}, bf16[512,640]{1,0:T(8,128)(2,1)S(1)}) fusion(bf16[512,3072]{1,0:T(8,128)(2,1)} %gather_attended.1, bf16[3072,640]{1,0:T(8,128)(2,1)} %get-tuple-element.17, bf16[512,5120]{1,0:T(8,128)(2,1)} %param.12, s32[]{:T(128)S(6)} %select_n.13), kind=kOutput, calls=%fused_computation.28 | convolution fusion | flops 2015231488 | bytes 8390660 | tf_op jit(solution)/shard_map/dot_general | solution.py:609
  178.9 0.8 dynamic-slice_convert_fusion
  179.7 0.3 fusion.36
  180.0 0.1 pad.2.clone
  180.1 0.7 maximum_maximum_fusion.a
  180.8 5.9 %gather_sums.1 = f32[64,512]{1,0:T(8,128)} custom-call(f32[8,512]{1,0:T(8,128)} %maximum_maximum_fusion.a), custom_call_target="tpu_custom_call" | custom-call | tf_op jit(solution)/shard_map/gather_sums/pallas_call | solution.py:445
  186.7 0.9 bitcast_reduce_fusion
  187.6 2.3 fusion.15.a
  189.9 27.9 %dispatch.1.a = bf16[1024,640]{1,0:T(8,128)(2,1)} custom-call(bf16[1024,640]{1,0:T(8,128)(2,1)} %fusion.15.a), custom_call_target="tpu_custom_call" | custom-call | tf_op jit(solution)/shard_map/dispatch/pallas_call | solution.py:485
  217.9 74.4 %gather_rows.1 = bf16[1024,5120]{1,0:T(8,128)(2,1)} custom-call(bf16[1024,640]{1,0:T(8,128)(2,1)} %dispatch.1.a), custom_call_target="tpu_custom_call" | custom-call | tf_op jit(solution)/shard_map/gather_rows/pallas_call | solution.py:131
  292.3 10.2 %fusion.3 = f32[1024,512]{1,0:T(8,128)S(1)} fusion(bf16[1024,5120]{1,0:T(8,128)(2,1)} %gather_rows.1, bf16[1,5120,512]{2,1,0:T(8,128)(2,1)} %param.22), kind=kOutput, calls=%fused_computation.5 | convolution fusion | flops 5368709120 | bytes 17825792 | tf_op jit(solution)/shard_map/dot_general | solution.py:641
  302.5 8.5 %multiply_convert_fusion.a = bf16[1024,512]{1,0:T(8,128)(2,1)} fusion(f32[1024,512]{1,0:T(8,128)S(1)} %fusion.3, bf16[1024,5120]{1,0:T(8,128)(2,1)S(1)} %copy-done.4, bf16[1,5120,512]{2,1,0:T(8,128)(2,1)} %param.21), kind=kOutput, calls=%fused_computation.17 | convolution fusion | flops 5371854848 | bytes 18874368 | tf_op jit(solution)/shard_map/dot_general | solution.py:640
  311.0 56.2 %gather_hidden.1 = bf16[1024,4096]{1,0:T(8,128)(2,1)} custom-call(bf16[1024,512]{1,0:T(8,128)(2,1)} %multiply_convert_fusion.a), custom_call_target="tpu_custom_call" | custom-call | tf_op jit(solution)/shard_map/gather_hidden/pallas_call | solution.py:131
  367.2 11.5 %convolution_convert_fusion.a = bf16[1024,640]{1,0:T(8,128)(2,1)} fusion(bf16[1024,4096]{1,0:T(8,128)(2,1)} %gather_hidden.1, bf16[4096,640]{1,0:T(8,128)(2,1)} %get-tuple-element.18), kind=kOutput, calls=%fused_computation.22 | convolution fusion | flops 5369364480 | bytes 14942208 | tf_op jit(solution)/shard_map/dot_general | solution.py:644
  378.7 27.2 %give_back.1 = bf16[1024,640]{1,0:T(8,128)(2,1)} custom-call(bf16[1024,640]{1,0:T(8,128)(2,1)} %convolution_convert_fusion.a), custom_call_target="tpu_custom_call" | custom-call | tf_op jit(solution)/shard_map/give_back/pallas_call | solution.py:485
  405.9 3.2 fusion.21
  (22 shorter events, 0.1 us)
Async XLA Ops:
  0.0 179.7 %copy-start = (bf16[5120,16]{0,1:T(8,128)(2,1)S(1)}, bf16[5120,16]{0,1:T(8,128)(2,1)}, u32[]{:S(2)}) copy-start(bf16[5120,16]{0,1:T(8,128)(2,1)} %param.19) | copy-start | bytes 491524
  0.0 7.9 %copy-start.6 = (bf16[320,128]{1,0:T(8,128)(2,1)S(1)}, bf16[320,128]{1,0:T(8,128)(2,1)}, u32[]{:S(2)}) copy-start(bf16[320,128]{1,0:T(8,128)(2,1)} %param.17) | copy-start | bytes 245764
  0.0 7.9 %copy-start.7 = (bf16[320,128]{1,0:T(8,128)(2,1)S(1)}, bf16[320,128]{1,0:T(8,128)(2,1)}, u32[]{:S(2)}) copy-start(bf16[320,128]{1,0:T(8,128)(2,1)} %param.16) | copy-start | bytes 245764
  0.0 7.9 %copy-start.5 = (bf16[320,384]{1,0:T(8,128)(2,1)S(1)}, bf16[320,384]{1,0:T(8,128)(2,1)}, u32[]{:S(2)}) copy-start(bf16[320,384]{1,0:T(8,128)(2,1)} %param.15) | copy-start | bytes 737284
  116.4 2.2 copy-start.3
  149.9 0.7 copy-start.2
  173.1 6.7 %copy-start.8 = (s32[512,1]{0,1:T(1,128)S(1)}, s32[512,1]{0,1:T(1,128)}, u32[]{:S(2)}) copy-start(s32[512,1]{0,1:T(1,128)} %param.20) | copy-start | bytes 6148
  292.3 10.2 %copy-start.4 = (bf16[1024,5120]{1,0:T(8,128)(2,1)S(1)}, bf16[1024,5120]{1,0:T(8,128)(2,1)}, u32[]{:S(2)}) copy-start(bf16[1024,5120]{1,0:T(8,128)(2,1)} %gather_rows.1) | copy-start | bytes 31457284
  367.2 41.9 %copy-start.1 = (bf16[5120,16]{0,1:T(8,128)(2,1)S(1)}, bf16[5120,16]{0,1:T(8,128)(2,1)}, u32[]{:S(2)}) copy-start(bf16[5120,16]{0,1:T(8,128)(2,1)} %param.19) | copy-start | bytes 491524

commit v3 on v2

--- a/solution.py
+++ b/solution.py
@@ -498,6 +498,241 @@
     )(a)
 
 
+class Gather:
+    def __init__(self, buf, row, rows, split, cols, sends, base):
+        z_hi, x, core, y, z_lo = place()
+        ctx = ctx_of(z_hi, x, core)
+        self.buf, self.cols, self.sends, self.base = buf, cols, sends, base
+        self.y, self.z, self.other = y, z_lo, 1 - z_lo
+        self.right, self.left, self.far = (y + 1) % 4, (y + 3) % 4, (y + 2) % 4
+        self.to_right, self.to_left = (ctx, self.right * 2 + z_lo), (ctx, self.left * 2 + z_lo)
+        self.to_z = (ctx, y * 2 + self.other)
+        half, rest = split // 2, rows - split
+        self.first, self.first_0, self.first_1 = (row, split), (row, half), (row + half, half)
+        self.rest, self.rest_0 = (row + split, rest), (row + split, rest // 2)
+        self.rest_1 = (row + split + rest // 2, rest // 2)
+
+    def at(self, y_of, z_of, part):
+        return self.buf.at[pl.ds(part[0], part[1]), pl.ds((y_of * 2 + z_of) * self.cols, self.cols)]
+
+    def go(self, k, y_of, z_of, part, device):
+        ref = self.at(y_of, z_of, part)
+        self.sends.start(self.base + k, ref, ref, device)
+
+    def got(self, k, y_of, z_of, part):
+        self.sends.arrived(self.base + k, self.at(y_of, z_of, part))
+
+    def own(self):
+        y, z = self.y, self.z
+        self.go(0, y, z, self.first, self.to_z)
+        self.go(1, y, z, self.first, self.to_right)
+        self.go(2, y, z, self.first, self.to_left)
+        self.go(3, y, z, self.rest, self.to_right)
+        self.go(4, y, z, self.rest, self.to_left)
+        self.go(5, y, z, self.rest, self.to_z)
+
+    def step_a(self):
+        self.got(0, self.y, self.other, self.first)
+        self.go(6, self.y, self.other, self.first, self.to_right)
+        self.go(7, self.y, self.other, self.first, self.to_left)
+
+    def step_b(self):
+        self.got(3, self.left, self.z, self.rest)
+        self.go(10, self.left, self.z, self.rest_0, self.to_right)
+        self.go(11, self.left, self.z, self.rest, self.to_z)
+        self.got(4, self.right, self.z, self.rest)
+        self.go(12, self.right, self.z, self.rest_1, self.to_left)
+        self.go(13, self.right, self.z, self.rest, self.to_z)
+
+    def step_c(self):
+        self.got(1, self.left, self.z, self.first)
+        self.go(8, self.left, self.z, self.first_0, self.to_right)
+        self.got(2, self.right, self.z, self.first)
+        self.go(9, self.right, self.z, self.first_1, self.to_left)
+
+    def step_d(self):
+        self.got(10, self.far, self.z, self.rest_0)
+        self.go(16, self.far, self.z, self.rest_0, self.to_z)
+        self.got(12, self.far, self.z, self.rest_1)
+        self.go(17, self.far, self.z, self.rest_1, self.to_z)
+
+    def step_e(self):
+        self.got(6, self.left, self.other, self.first)
+        self.go(14, self.left, self.other, self.first_0, self.to_right)
+        self.got(7, self.right, self.other, self.first)
+        self.go(15, self.right, self.other, self.first_1, self.to_left)
+
+    def finish(self):
+        self.got(5, self.y, self.other, self.rest)
+        self.got(8, self.far, self.z, self.first_0)
+        self.got(9, self.far, self.z, self.first_1)
+        self.got(11, self.left, self.other, self.rest)
+        self.got(13, self.right, self.other, self.rest)
+        self.got(14, self.far, self.other, self.first_0)
+        self.got(15, self.far, self.other, self.first_1)
+        self.got(16, self.far, self.other, self.rest_0)
+        self.got(17, self.far, self.other, self.rest_1)
+
+
+PARTS = 2
+
+
+def experts_kernel(
+    buffer, w_gate, w_up, down_cols, out, rows, hidden, done, gate_v, up_v, down_v, local_sem, send_sem, recv_sem
+):
+    z_hi, x, core, y, z_lo = place()
+    me, hx = ctx_of(z_hi, x, core), y * 2 + z_lo
+    width, deep = buffer.shape[1], w_gate.shape[1]
+    total = buffer.shape[0]
+    chunk = total // PARTS
+    slot = chunk // 16
+    loads = (
+        pltpu.make_async_copy(w_gate, gate_v, local_sem.at[0]),
+        pltpu.make_async_copy(w_up, up_v, local_sem.at[1]),
+        pltpu.make_async_copy(down_cols, down_v, local_sem.at[2]),
+    )
+    mine = pl.ds(hx * width, width)
+    keeps = [
+        pltpu.make_async_copy(
+            buffer.at[pl.ds(c * chunk + me * slot, slot), :],
+            rows.at[pl.ds(c * chunk + me * slot, slot), mine],
+            local_sem.at[3 + c],
+        )
+        for c in range(PARTS)
+    ]
+    for copy in keeps:
+        copy.start()
+    near = ((y + 1) % 4 * 2 + z_lo, (y + 3) % 4 * 2 + z_lo, y * 2 + 1 - z_lo)
+    greet([((me + k) % 16, hx) for k in range(1, 16)] + [(me, p) for p in near])
+    sends = Sends(send_sem, recv_sem)
+
+    def spot(c, p):
+        return pl.ds(c * chunk + p * slot, slot)
+
+    def dispatch(c):
+        for k in range(1, 16):
+            peer = (me + k) % 16
+            sends.start(c * 15 + k - 1, buffer.at[spot(c, peer), :], rows.at[spot(c, me), mine], (peer, hx))
+
+    def dispatched(c):
+        keeps[c].wait()
+        for k in range(1, 16):
+            sends.arrived(c * 15 + k - 1, rows.at[spot(c, (me + 16 - k) % 16), mine])
+
+    def give(c):
+        base = PARTS * 15
+        for k in range(1, 16):
+            peer = (me + k) % 16
+            sends.start(base + c * 15 + k - 1, done.at[spot(c, peer), :], out.at[spot(c, me), :], (peer, hx))
+        keep = pltpu.make_async_copy(done.at[spot(c, me), :], out.at[spot(c, me), :], local_sem.at[3 + PARTS + c])
+        keep.start()
+        keeps.append(keep)
+
+    def given(c):
+        base = PARTS * 15
+        for k in range(1, 16):
+            sends.arrived(base + c * 15 + k - 1, out.at[spot(c, (me + 16 - k) % 16), :])
+
+    def hide(c, n):
+        step = 256
+        r, f = pl.ds(c * chunk, chunk), pl.ds(n * step, step)
+        gate = jnp.dot(rows[r, :], gate_v[:, f], preferred_element_type=jnp.float32)
+        up = jnp.dot(rows[r, :], up_v[:, f], preferred_element_type=jnp.float32)
+        spread = pl.ds(pl.multiple_of(hx * deep + n * step, step), step)
+        hidden[r, spread] = (gate * jax.nn.sigmoid(gate) * up).astype(hidden.dtype)
+
+    def lower(c):
+        r = pl.ds(c * chunk, chunk)
+        for at, step in ((0, 256), (256, 256), (512, 128)):
+            f = pl.ds(at, step)
+            done[r, f] = jnp.dot(hidden[r, :], down_v[:, f], preferred_element_type=jnp.float32).astype(done.dtype)
+
+    base = PARTS * 30
+    split = chunk * 9 // 16 // 32 * 32
+    row_gathers = [Gather(rows, c * chunk, chunk, split, width, sends, base + 18 * c) for c in range(PARTS)]
+    base += 18 * PARTS
+    hid_gathers = [Gather(hidden, c * chunk, chunk, split, deep, sends, base + 18 * c) for c in range(PARTS)]
+    r0, r1 = row_gathers
+    h0, h1 = hid_gathers
+
+    for c in range(PARTS):
+        dispatch(c)
+    for load in loads:
+        load.start()
+    dispatched(0)
+    r0.own()
+    r0.step_a()
+    r0.step_b()
+    dispatched(1)
+    r1.own()
+    r0.step_c()
+    r0.step_d()
+    r0.step_e()
+    r1.step_a()
+    r1.step_b()
+    r0.finish()
+    for load in loads:
+        load.wait()
+    hide(0, 0)
+    r1.step_c()
+    r1.step_d()
+    hide(0, 1)
+    r1.step_e()
+    h0.own()
+    r1.finish()
+    hide(1, 0)
+    h0.step_a()
+    h0.step_b()
+    hide(1, 1)
+    h0.step_c()
+    h1.own()
+    h0.step_d()
+    h0.step_e()
+    h1.step_a()
+    h1.step_b()
+    h0.finish()
+    lower(0)
+    h1.step_c()
+    h1.step_d()
+    give(0)
+    h1.step_e()
+    h1.finish()
+    lower(1)
+    given(0)
+    give(1)
+    given(1)
+    sends.drain()
+    for keep in keeps[PARTS:]:
+        keep.wait()
+
+
+def run_experts(buffer, w_gate, w_up, down_cols, call_id):
+    total, width = buffer.shape
+    full, deep = w_gate.shape
+    copies = PARTS * 66
+    return pl.pallas_call(
+        experts_kernel,
+        out_shape=jax.ShapeDtypeStruct((total, width), buffer.dtype),
+        in_specs=[ANY] * 4,
+        out_specs=ANY,
+        scratch_shapes=[
+            pltpu.VMEM((total, full), buffer.dtype),
+            pltpu.VMEM((total, deep * 8), buffer.dtype),
+            pltpu.VMEM((total, width), buffer.dtype),
+            pltpu.VMEM((full, deep), buffer.dtype),
+            pltpu.VMEM((full, deep), buffer.dtype),
+            pltpu.VMEM((deep * 8, width), buffer.dtype),
+            pltpu.SemaphoreType.DMA((3 + 2 * PARTS,)),
+            pltpu.SemaphoreType.DMA((copies,)),
+            pltpu.SemaphoreType.DMA((copies,)),
+        ],
+        compiler_params=pltpu.CompilerParams(
+            collective_id=call_id, has_side_effects=True, vmem_limit_bytes=60 << 20
+        ),
+        name="experts",
+    )(buffer, w_gate, w_up, down_cols)
+
+
 def attend_kernel(q_t, kv, w_down, _, out, down_cols, send_sem, recv_sem):
     me, hx = lax.axis_index("ctx"), lax.axis_index("hx")
     y, z_lo = hx // 2, hx % 2
@@ -619,7 +854,8 @@
     capacity = tok_rows // 8
     counts = jnp.cumsum(onehot.astype(jnp.int32), axis=0)
     position = jnp.sum(jnp.where(onehot, counts, 0), axis=-1) - 1
-    slot = chosen * capacity + position
+    slots = capacity // PARTS
+    slot = position // slots * (experts * slots) + chosen * slots + position % slots
     picks = (slot[None, :] == jnp.arange(experts * capacity, dtype=jnp.int32)[:, None]).astype(bf16)
 
     gained = stream_f * own_gain
@@ -635,14 +871,7 @@
     normed2 = (stream_f * inverse2 * own_gain).astype(bf16)
     routed = (normed2.astype(f32) * score).astype(bf16)
     buffer = jnp.dot(picks, routed, preferred_element_type=f32).astype(bf16)
-    arrived = ctx_exchange(buffer, 6, "dispatch")
-    rows = hx_gather(arrived, 1, "gather_rows")
-    gate = jnp.dot(rows, w_gate[0], preferred_element_type=f32)
-    up = jnp.dot(rows, w_up[0], preferred_element_type=f32)
-    hidden = (jax.nn.silu(gate) * up).astype(bf16)
-    hidden_all = hx_gather(hidden, 8, "gather_hidden")
-    expert_rows = jnp.dot(hidden_all, down_cols, preferred_element_type=f32).astype(bf16)
-    returned = ctx_exchange(expert_rows, 9, "give_back")
+    returned = run_experts(buffer, w_gate[0], w_up[0], down_cols, 6)
     expert_out = lax.dot_general(picks, returned, (((0,), (0,)), ((), ())), preferred_element_type=f32)
     return (stream_f + expert_out.astype(bf16).astype(f32)).astype(bf16)
 

time: 410 us -> 360 us (0.88)
  matrix products: 53.5 us -> 23.4 us
  Pallas kernels: 341 us -> 322 us
    pallas_call x3 -> x1, Pallas kernels: 153 us -> 22.5 us  [hx_gather(): pl.pallas_call(functools.partial(hx_gather_kernel, rows, cols, split), ou...]
    pallas_call x2 -> x1, Pallas kernels: 55.1 us -> 166 us  [run_experts(): pl.pallas_call(experts_kernel, out_shape=jax.ShapeDtypeStruct((total, wid...]
    dot_general x3 -> x0, matrix products: 30.2 us -> none  [the longest x1 11.5 us: body(): jnp.dot(hidden_all, down_cols, preferred_element_type=f32).astype(bf16)]
where the time goes in v3:
time: 360 us
  Pallas kernels  322 us (89%)
  matrix products  23.4 us (6%)
  other arithmetic  10.9 us (3%)
    pallas_call x1, Pallas kernels, run_experts(): pl.pallas_call(experts_kernel, out_shape=jax.ShapeDtypeStruct((total, wid...  166 us
    pallas_call x1, Pallas kernels, gather_weights(): pl.pallas_call(functools.partial(gather_weights_kernel, rows), out_shape=...  57.9 us
    pallas_call x1, Pallas kernels, gather_kv(): pl.pallas_call(functools.partial(gather_kv_kernel, rows), out_shape=(jax....  38.2 us
    pallas_call x1, Pallas kernels, attend(): pl.pallas_call(attend_kernel, out_shape=(jax.ShapeDtypeStruct((tok, cols)...  31.3 us
    pallas_call x1, Pallas kernels, hx_gather(): pl.pallas_call(functools.partial(hx_gather_kernel, rows, cols, split), ou...  22.5 us

profile of v3, /device:TPU:1, one launch (start us, length us, event | category | flops | bytes accessed | tf_op | source)
XLA Modules:
  0.0 359.7 jit_solution(7229484185381822254)
XLA Ops:
  0.0 0.0 copy-start
  0.0 0.0 copy-start.3
  0.0 0.7 fusion.41
  0.8 1.1 reduce-window.6
  1.9 0.2 slice_reduce_fusion
  2.2 0.8 fusion.40
  2.9 0.7 fusion.45
  3.6 0.7 convert_element_type.59
  4.3 3.6 fusion
  7.9 0.0 copy-done.5
  8.0 0.0 copy-done.3
  8.0 0.8 pad_maximum_fusion.a
  8.8 57.9 %gather_weights.1 = (bf16[5120,640]{1,0:T(8,128)(2,1)}, bf16[2,160,640]{2,1,0:T(8,128)(2,1)}, bf16[3072,640]{1,0:T(8,128)(2,1)}, bf16[4096,640]{1,0:T(8,128)(2,1)}) custom-call(bf16[320,640]{1,0:T(8,128)(2,1)} %pad_maximum_fusion.a, bf16[384,5120]{1,0:T(8,128)(2,1)} %w_out.1, bf16[512,5120]{1,0:T(8,128)(2,1)} %bitcast.29), custom_call_target="tpu_custom_call" | custom-call | tf_op jit(solution)/shard_map/gather_weights/pallas_call | solution.py:315
  66.7 6.0 %fusion.20.q_t = bf16[384,512]{1,0:T(8,128)(2,1)S(1)} fusion(bf16[512,5120]{1,0:T(8,128)(2,1)} %param.12, f32[5120]{0:T(1024)S(1)} %convert_element_type.59, f32[512]{0:T(512)S(1)} %add_rsqrt_fusion, bf16[5120,640]{1,0:T(8,128)(2,1)} %get-tuple-element.12), kind=kOutput, calls=%fused_computation.27 | convolution fusion | flops 2023948288 | bytes 9590784 | tf_op jit(solution)/shard_map/td,dc->ct/dot_general | solution.py:838
  72.7 5.6 %fusion.25.a = bf16[512,256]{1,0:T(8,128)(2,1)} fusion(bf16[5120,640]{1,0:T(8,128)(2,1)} %get-tuple-element.12, bf16[512,5120]{1,0:T(8,128)(2,1)} %param.12, f32[5120]{0:T(1024)S(1)} %convert_element_type.59, f32[512]{0:T(512)S(1)} %add_rsqrt_fusion), kind=kOutput, calls=%fused_computation.28 | convolution fusion | flops 1352794112 | bytes 8148992 | tf_op jit(solution)/shard_map/dot_general | solution.py:839
  78.3 38.2 %gather_kv.1 = (bf16[8192,256]{1,0:T(8,128)(2,1)}, bf16[2,256,256]{2,1,0:T(8,128)(2,1)}, bf16[4,256,640]{2,1,0:T(8,128)(2,1)}, bf16[4096,640]{1,0:T(8,128)(2,1)}) custom-call(bf16[512,256]{1,0:T(8,128)(2,1)} %fusion.25.a, bf16[512,5120]{1,0:T(8,128)(2,1)} %bitcast.30, bf16[4096,640]{1,0:T(8,128)(2,1)} %get-tuple-element.13._), custom_call_target="tpu_custom_call", output_to_operand_aliasing={{3}: (2, {})} | custom-call | tf_op jit(solution)/shard_map/gather_kv/pallas_call | solution.py:398
  116.5 2.2 copy-done.2
  118.6 31.3 %attend.1 = (bf16[512,384]{1,0:T(8,128)(2,1)S(1)}, bf16[4096,640]{1,0:T(8,128)(2,1)}) custom-call(bf16[384,512]{1,0:T(8,128)(2,1)S(1)} %fusion.20.q_t, bf16[8192,256]{1,0:T(8,128)(2,1)S(1)} %copy-done.2, bf16[512,5120]{1,0:T(8,128)(2,1)} %bitcast.31, bf16[4096,640]{1,0:T(8,128)(2,1)} %get-tuple-element.15._), custom_call_target="tpu_custom_call", output_to_operand_aliasing={{1}: (3, {})} | custom-call | flops 6442450944 | bytes 4194304 | tf_op jit(solution)/shard_map/attend/pallas_call | solution.py:801
  149.9 0.0 copy-start.1
  149.9 0.7 copy-done.1
  150.7 22.5 %gather_attended.1 = bf16[512,3072]{1,0:T(8,128)(2,1)} custom-call(bf16[512,384]{1,0:T(8,128)(2,1)} %copy-done.1), custom_call_target="tpu_custom_call" | custom-call | tf_op jit(solution)/shard_map/gather_attended/pallas_call | solution.py:131
  173.2 0.0 copy-start.6
  173.2 6.0 %fusion.16 = (f32[512]{0:T(512)S(1)}, bf16[512,640]{1,0:T(8,128)(2,1)S(1)}) fusion(bf16[512,3072]{1,0:T(8,128)(2,1)} %gather_attended.1, bf16[3072,640]{1,0:T(8,128)(2,1)} %get-tuple-element.17, bf16[512,5120]{1,0:T(8,128)(2,1)} %param.12, s32[]{:T(128)S(6)} %select_n.33), kind=kOutput, calls=%fused_computation.22 | convolution fusion | flops 2015231488 | bytes 8390660 | tf_op jit(solution)/shard_map/dot_general | solution.py:844
  179.2 0.8 dynamic-slice_convert_fusion
  179.9 0.3 fusion.30
  180.2 0.1 pad.2.clone
  180.3 0.7 maximum_maximum_fusion.a
  181.0 5.9 %gather_sums.1 = f32[64,512]{1,0:T(8,128)} custom-call(f32[8,512]{1,0:T(8,128)} %maximum_maximum_fusion.a), custom_call_target="tpu_custom_call" | custom-call | tf_op jit(solution)/shard_map/gather_sums/pallas_call | solution.py:445
  186.9 0.9 bitcast_reduce_fusion
  187.8 2.3 fusion.9.buffer
  190.1 166.3 %experts.1 = bf16[1024,640]{1,0:T(8,128)(2,1)} custom-call(bf16[1024,640]{1,0:T(8,128)(2,1)} %fusion.9.buffer, bf16[5120,512]{1,0:T(8,128)(2,1)} %bitcast.32, bf16[5120,512]{1,0:T(8,128)(2,1)} %bitcast.33, bf16[4096,640]{1,0:T(8,128)(2,1)} %get-tuple-element.18.down_cols), custom_call_target="tpu_custom_call" | custom-call | tf_op jit(solution)/shard_map/experts/pallas_call | solution.py:713
  356.5 3.2 fusion.15
  (12 shorter events, 0.1 us)
Async XLA Ops:
  0.0 179.9 %copy-start = (bf16[5120,16]{0,1:T(8,128)(2,1)S(1)}, bf16[5120,16]{0,1:T(8,128)(2,1)}, u32[]{:S(2)}) copy-start(bf16[5120,16]{0,1:T(8,128)(2,1)} %param.19) | copy-start | bytes 491524
  0.0 7.9 %copy-start.4 = (bf16[320,128]{1,0:T(8,128)(2,1)S(1)}, bf16[320,128]{1,0:T(8,128)(2,1)}, u32[]{:S(2)}) copy-start(bf16[320,128]{1,0:T(8,128)(2,1)} %param.17) | copy-start | bytes 245764
  0.0 7.9 %copy-start.5 = (bf16[320,128]{1,0:T(8,128)(2,1)S(1)}, bf16[320,128]{1,0:T(8,128)(2,1)}, u32[]{:S(2)}) copy-start(bf16[320,128]{1,0:T(8,128)(2,1)} %param.16) | copy-start | bytes 245764
  0.0 8.0 %copy-start.3 = (bf16[320,384]{1,0:T(8,128)(2,1)S(1)}, bf16[320,384]{1,0:T(8,128)(2,1)}, u32[]{:S(2)}) copy-start(bf16[320,384]{1,0:T(8,128)(2,1)} %param.15) | copy-start | bytes 737284
  116.5 2.2 copy-start.2
  149.9 0.7 copy-start.1
  173.2 6.8 %copy-start.6 = (s32[512,1]{0,1:T(1,128)S(1)}, s32[512,1]{0,1:T(1,128)}, u32[]{:S(2)}) copy-start(s32[512,1]{0,1:T(1,128)} %param.20) | copy-start | bytes 6148

commit v4 on v0

v4 whole, which is shorter than its diff:
```python
import functools
import math
import jax
import jax.numpy as jnp
from jax import lax
from jax.experimental import pallas as pl
from jax.experimental.pallas import tpu as pltpu
from jax.sharding import PartitionSpec as P

HD = 128
epsilon = 1e-05
MESH = pl.DeviceIdType.MESH


def place():
    ctx, hx = lax.axis_index("ctx"), lax.axis_index("hx")
    z_hi, x, core = ctx // 8, (ctx // 2) % 4, ctx % 2
    y, z_lo = hx // 2, hx % 2
    return z_hi, x, core, y, z_lo


def ctx_of(z_hi, x, core):
    return z_hi * 8 + x * 2 + core


def greet(devices):
    barrier = pltpu.get_barrier_semaphore()
    for device in devices:
        pl.semaphore_signal(barrier, inc=1, device_id=device, device_id_type=MESH)
    pl.semaphore_wait(barrier, len(devices))


class Sends:
    def __init__(self, send_sem, recv_sem):
        self.send_sem, self.recv_sem, self.started = send_sem, recv_sem, []

    def start(self, k, src, dst, device):
        copy = pltpu.make_async_remote_copy(
            src_ref=src,
            dst_ref=dst,
            send_sem=self.send_sem.at[k],
            recv_sem=self.recv_sem.at[k],
            device_id=device,
            device_id_type=MESH,
        )
        copy.start()
        self.started.append(copy)

    def arrived(self, k, dst):
        pltpu.make_async_copy(dst, dst, self.recv_sem.at[k]).wait()

    def drain(self):
        for copy in self.started:
            copy.wait_send()


def ctx_neighbours():
    z_hi, x, core, y, z_lo = place()
    hx = y * 2 + z_lo
    z = z_hi * 2 + z_lo
    up, down = (z + 1) % 4, (z + 3) % 4
    return (
        (ctx_of(z_hi, (x + 1) % 4, core), hx),
        (ctx_of(z_hi, (x + 3) % 4, core), hx),
        (ctx_of(up // 2, x, core), y * 2 + up % 2),
        (ctx_of(down // 2, x, core), y * 2 + down % 2),
        (ctx_of(z_hi, x, 1 - core), hx),
    )


class Spread:
    def __init__(self, own, out, transit, rows, sends, base):
        z_hi, x, core, y, z_lo = place()
        hx = y * 2 + z_lo
        z = z_hi * 2 + z_lo
        up, down = (z + 1) % 4, (z + 3) % 4
        self.own_ref, self.out, self.transit, self.rows, self.sends, self.base = own, out, transit, rows, sends, base
        self.z, self.x, self.core, self.other = z_hi, x, core, 1 - z_hi
        self.right, self.left, self.far = (x + 1) % 4, (x + 3) % 4, (x + 2) % 4
        self.z_up, self.z_down = up // 2, down // 2
        self.to_right, self.to_left = (ctx_of(z_hi, self.right, core), hx), (ctx_of(z_hi, self.left, core), hx)
        self.to_up = (ctx_of(up // 2, x, core), y * 2 + up % 2)
        self.to_down = (ctx_of(down // 2, x, core), y * 2 + down % 2)
        self.to_core = (ctx_of(z_hi, x, 1 - core), hx)
        self.whole, self.half_0, self.half_1 = (0, rows), (0, rows // 2), (rows // 2, rows // 2)

    def at(self, z_of, x_of, core_of, part):
        return self.out.at[pl.ds(ctx_of(z_of, x_of, core_of) * self.rows + part[0], part[1]), :]

    def go(self, k, z_of, x_of, part, device):
        ref = self.at(z_of, x_of, self.core, part)
        self.sends.start(self.base + k, ref, ref, device)

    def got(self, k, z_of, x_of, part):
        self.sends.arrived(self.base + k, self.at(z_of, x_of, self.core, part))

    def from_core(self, k, z_of, x_of):
        self.sends.arrived(self.base + k, self.at(z_of, x_of, 1 - self.core, self.whole))

    def start(self):
        def own(part):
            return self.own_ref.at[pl.ds(part[0], part[1]), :]

        here = self.at(self.z, self.x, self.core, self.whole)
        self.sends.start(self.base + 0, own(self.half_0), self.transit.at[0], self.to_up)
        self.sends.start(self.base + 1, own(self.half_1), self.transit.at[1], self.to_down)
        self.sends.start(self.base + 2, own(self.whole), here, self.to_right)
        self.sends.start(self.base + 3, own(self.whole), here, self.to_left)
        self.sends.start(self.base + 4, own(self.whole), here, self.to_core)

    def pass_z(self):
        self.sends.arrived(self.base + 0, self.transit.at[0])
        self.sends.start(
            self.base + 5, self.transit.at[0], self.at(self.z_down, self.x, self.core, self.half_0), self.to_up
        )
        self.sends.arrived(self.base + 1, self.transit.at[1])
        self.sends.start(
            self.base + 6, self.transit.at[1], self.at(self.z_up, self.x, self.core, self.half_1), self.to_down
        )

    def pass_near(self):
        self.got(2, self.z, self.left, self.whole)
        self.go(10, self.z, self.left, self.half_0, self.to_right)
        self.go(11, self.z, self.left, self.whole, self.to_core)
        self.got(3, self.z, self.right, self.whole)
        self.go(12, self.z, self.right, self.half_1, self.to_left)
        self.go(13, self.z, self.right, self.whole, self.to_core)

    def pass_other(self):
        self.got(5, self.other, self.x, self.half_0)
        self.got(6, self.other, self.x, self.half_1)
        self.go(7, self.other, self.x, self.whole, self.to_right)
        self.go(8, self.other, self.x, self.whole, self.to_left)
        self.go(9, self.other, self.x, self.whole, self.to_core)

    def pass_far(self):
        self.got(10, self.z, self.far, self.half_0)
        self.got(12, self.z, self.far, self.half_1)
        self.go(18, self.z, self.far, self.whole, self.to_core)

    def pass_other_near(self):
        self.got(7, self.other, self.left, self.whole)
        self.go(14, self.other, self.left, self.half_0, self.to_right)
        self.go(15, self.other, self.left, self.whole, self.to_core)
        self.got(8, self.other, self.right, self.whole)
        self.go(16, self.other, self.right, self.half_1, self.to_left)
        self.go(17, self.other, self.right, self.whole, self.to_core)

    def pass_other_far(self):
        self.got(14, self.other, self.far, self.half_0)
        self.got(16, self.other, self.far, self.half_1)
        self.go(19, self.other, self.far, self.whole, self.to_core)


def front_kernel(
    tokens, gain, a, w_out, w_down, attended, out_cols, down_cols,
    normed, weights, transit_w, kv, transit_kv, passing, held_out, held_down, sums, q_t, top_v, total_v, acc_v,
    local_sem, send_sem, recv_sem,
):
    z_hi, x, core, y, z_lo = place()
    ctx, me = ctx_of(z_hi, x, core), y * 2 + z_lo
    other = 1 - z_hi
    tok, full = tokens.shape
    rows = a.shape[0]
    q_cols = q_t.shape[0]
    heads = q_cols // HD
    width, deep = held_out.shape[1], w_down.shape[0]
    half = deep // 2
    sub, piece = x * 2 + core, out_cols.shape[2]
    mine = pl.ds(me * width, width)
    loads = (
        pltpu.make_async_copy(tokens, normed, local_sem.at[0]),
        pltpu.make_async_copy(a, weights.at[pl.ds(ctx * rows, rows), :], local_sem.at[1]),
        pltpu.make_async_copy(w_out.at[pl.ds(sub * piece, piece), mine], held_out, local_sem.at[2]),
        pltpu.make_async_copy(w_down.at[:, mine], held_down, local_sem.at[3]),
    )
    for load in loads:
        load.start()
    greet(ctx_neighbours() + tuple((ctx, (me + k) % 8) for k in range(1, 8)))
    sends = Sends(send_sem, recv_sem)

    def peer_of(y_step, flip):
        return (y + y_step) % 4 * 2 + (1 - z_lo if flip else z_lo)

    order = ((1, 0), (3, 0), (2, 0), (0, 1), (1, 1), (3, 1), (2, 1))

    def share(i):
        peer = peer_of(*order[i])
        src = w_out.at[pl.ds(sub * piece, piece), pl.ds(peer * width, width)]
        sends.start(40 + i, src, out_cols.at[me, sub], (ctx, peer))

    right, left, far = (x + 1) % 4, (x + 3) % 4, (x + 2) % 4
    to_right, to_left = (ctx_of(z_hi, right, core), me), (ctx_of(z_hi, left, core), me)
    to_core = (ctx_of(z_hi, x, 1 - core), me)
    whole, half_0, half_1 = (0, 8), (0, 4), (4, 4)

    def of_chip(x_of, core_of, part):
        return out_cols.at[pl.ds(part[0], part[1]), x_of * 2 + core_of]

    def pass_out(k, x_of, part, device):
        block = of_chip(x_of, core, part)
        sends.start(k, block, block, device)

    def ring_start():
        for i in range(7):
            y_step, flip = order[i]
            sends.arrived(40 + i, out_cols.at[peer_of(4 - y_step, flip), sub])
        keep_out.wait()
        pass_out(47, x, whole, to_right)
        pass_out(48, x, whole, to_left)
        pass_out(49, x, whole, to_core)

    def ring_near():
        sends.arrived(47, of_chip(left, core, whole))
        pass_out(50, left, half_0, to_right)
        pass_out(51, left, whole, to_core)
        sends.arrived(48, of_chip(right, core, whole))
        pass_out(52, right, half_1, to_left)
        pass_out(53, right, whole, to_core)

    def ring_far():
        sends.arrived(50, of_chip(far, core, half_0))
        sends.arrived(52, of_chip(far, core, half_1))
        pass_out(67, far, whole, to_core)
        for k, x_of in ((49, x), (51, left), (53, right), (67, far)):
            sends.arrived(k, of_chip(x_of, 1 - core, whole))

    def down_rows(source, h, count):
        return down_cols.at[pl.ds(source * deep + h * half, count), :]

    def down_block(k, peer):
        sends.start(k, w_down.at[:, pl.ds(peer * width, width)], down_rows(me, 0, deep), (ctx, peer))

    def first_hop():
        for k, h, flip, step in ((55, 0, 0, 1), (57, 1, 0, 3), (56, 0, 1, 1), (58, 1, 1, 3)):
            src = w_down.at[pl.ds(h * half, half), pl.ds(peer_of(2, flip) * width, width)]
            sends.start(k, src, passing.at[k - 55], (ctx, peer_of(step, 0)))

    def second_hop(flip):
        for k, h, step in ((55 + flip, 0, 1), (57 + flip, 1, 3)):
            sends.arrived(k, passing.at[k - 55])
            source = peer_of(4 - step, 0)
            sends.start(k + 4, passing.at[k - 55], down_rows(source, h, half), (ctx, peer_of(step, flip)))

    spread_w = Spread(a, weights, transit_w, rows, sends, 0)
    spread_w.start()
    for i in range(3):
        share(i)

    loads[0].wait()
    loads[2].wait()
    keep_out = pltpu.make_async_copy(held_out, out_cols.at[me, sub], local_sem.at[4])
    keep_out.start()

    def norm(i, carry):
        r = pl.ds(pl.multiple_of(i * 64, 64), 64)
        floats = normed[r, :].astype(jnp.float32)
        inverse = lax.rsqrt(jnp.mean(floats * floats, axis=-1, keepdims=True) + epsilon)
        normed[r, :] = (floats * inverse * gain[...]).astype(normed.dtype)
        return carry

    lax.fori_loop(0, tok // 64, norm, 0)
    sums[...] = jnp.zeros_like(sums)

    def project(z_of, x_of):
        at = pl.multiple_of(ctx_of(z_of, x_of, 0) * rows, 2 * rows)
        sums[...] += jnp.dot(
            normed[:, pl.ds(at, 2 * rows)], weights[pl.ds(at, 2 * rows), :], preferred_element_type=jnp.float32
        )

    def two(visit):
        return lambda j, carry: (visit(j), carry)[1]

    spread_w.pass_z()
    for i in range(3, 7):
        share(i)
    down_block(54, peer_of(0, 1))
    first_hop()
    down_block(63, peer_of(1, 0))
    down_block(64, peer_of(3, 0))
    spread_w.pass_near()
    loads[1].wait()
    spread_w.from_core(4, z_hi, x)
    project(z_hi, x)
    spread_w.pass_other()
    spread_w.from_core(11, z_hi, spread_w.left)
    spread_w.from_core(13, z_hi, spread_w.right)
    lax.fori_loop(0, 2, two(lambda j: project(z_hi, (x + 1 + 2 * j) % 4)), 0)
    spread_w.pass_far()
    spread_w.from_core(9, other, x)
    project(other, x)
    spread_w.pass_other_near()
    spread_w.from_core(18, z_hi, spread_w.far)
    project(z_hi, spread_w.far)
    spread_w.from_core(15, other, spread_w.left)
    spread_w.from_core(17, other, spread_w.right)
    lax.fori_loop(0, 2, two(lambda j: project(other, (x + 1 + 2 * j) % 4)), 0)
    spread_w.pass_other_far()
    spread_w.from_core(19, other, spread_w.far)
    project(other, spread_w.far)

    own_rows = pl.ds(ctx * tok, tok)
    kv[own_rows, :] = sums[:, q_cols:].astype(kv.dtype)
    for h in range(heads):
        q_t[h * HD : (h + 1) * HD, :] = sums[:, h * HD : (h + 1) * HD].T.astype(q_t.dtype)
    top_v[...] = jnp.full_like(top_v, -1e30)
    total_v[...] = jnp.zeros_like(total_v)
    acc_v[...] = jnp.zeros_like(acc_v)
    scale = HD ** (-0.5) * math.log2(math.e)

    def visit(block, diagonal):
        at = pl.multiple_of(block * tok, tok)
        keys = kv[pl.ds(at, tok), :HD]
        values = kv[pl.ds(at, tok), HD:]
        for h in range(heads):
            r = slice(h * HD, (h + 1) * HD)
            top, total = top_v[h : h + 1, :], total_v[h : h + 1, :]
            scores = jnp.dot(keys, q_t[r, :], preferred_element_type=jnp.float32) * scale
            if diagonal:
                key_pos = lax.broadcasted_iota(jnp.int32, scores.shape, 0)
                query_pos = lax.broadcasted_iota(jnp.int32, scores.shape, 1)
                scores = jnp.where(key_pos <= query_pos, scores, -1e30)
            new_top = jnp.maximum(top, jnp.max(scores, axis=0, keepdims=True))
            weight = jnp.exp2(scores - new_top)
            factor = jnp.exp2(top - new_top)
            top_v[h : h + 1, :] = new_top
            total_v[h : h + 1, :] = total * factor + jnp.sum(weight, axis=0, keepdims=True)
            mixed = lax.dot_general(
                values, weight.astype(jnp.bfloat16), (((0,), (0,)), ((), ())), preferred_element_type=jnp.float32
            )
            acc_v[r, :] = acc_v[r, :] * factor + mixed

    def seen(block):
        @pl.when(block < ctx)
        def _():
            visit(block, False)

    spread_kv = Spread(kv.at[own_rows, :], kv, transit_kv, tok, sends, 20)
    spread_kv.start()
    visit(ctx, True)
    spread_kv.pass_z()
    down_block(65, peer_of(1, 1))
    down_block(66, peer_of(3, 1))
    spread_kv.pass_near()
    second_hop(0)
    spread_kv.pass_other()
    spread_kv.from_core(4, z_hi, x)
    seen(ctx_of(z_hi, x, 1 - core))
    spread_kv.from_core(11, z_hi, spread_kv.left)
    spread_kv.from_core(13, z_hi, spread_kv.right)
    lax.fori_loop(0, 4, two(lambda j: seen(ctx_of(z_hi, (x + 1 + j // 2 * 2) % 4, j % 2))), 0)
    spread_kv.pass_far()
    spread_kv.pass_other_near()
    ring_start()
    second_hop(1)
    spread_kv.from_core(9, other, x)
    spread_kv.from_core(18, z_hi, spread_kv.far)
    lax.fori_loop(0, 4, two(lambda j: seen(ctx_of((z_hi + 1 - j // 2) % 2, (x + j // 2 * 2) % 4, j % 2))), 0)
    spread_kv.pass_other_far()
    ring_near()
    spread_kv.from_core(15, other, spread_kv.left)
    spread_kv.from_core(17, other, spread_kv.right)
    spread_kv.from_core(19, other, spread_kv.far)
    lax.fori_loop(0, 6, two(lambda j: seen(ctx_of(other, (x + 1 + j // 2) % 4, j % 2))), 0)
    for h in range(heads):
        r = slice(h * HD, (h + 1) * HD)
        attended[:, r] = (acc_v[r, :] / total_v[h : h + 1, :]).T.astype(attended.dtype)

    loads[3].wait()
    keep_down = pltpu.make_async_copy(held_down, down_rows(me, 0, deep), local_sem.at[5])
    keep_down.start()
    ring_far()
    sends.arrived(54, down_rows(peer_of(0, 1), 0, deep))
    for flip in (0, 1):
        sends.arrived(59 + flip, down_rows(peer_of(2, flip), 0, half))
        sends.arrived(61 + flip, down_rows(peer_of(2, flip), 1, half))
    for k, y_step, flip in ((63, 1, 0), (64, 3, 0), (65, 1, 1), (66, 3, 1)):
        sends.arrived(k, down_rows(peer_of(4 - y_step, flip), 0, deep))
    sends.drain()
    keep_down.wait()


ANY = pl.BlockSpec(memory_space=pl.ANY)
VMEM = pl.BlockSpec(memory_space=pltpu.VMEM)


def run_front(tokens, gain, a, w_out, w_down, q_cols, call_id):
    bf16, f32 = jnp.bfloat16, jnp.float32
    tok, full = tokens.shape
    rows, cols = a.shape
    depth, deep, width = w_out.shape[0], w_down.shape[0], full // 8
    return pl.pallas_call(
        front_kernel,
        out_shape=(
            jax.ShapeDtypeStruct((tok, q_cols), bf16),
            jax.ShapeDtypeStruct((8, 8, depth // 8, width), bf16),
            jax.ShapeDtypeStruct((deep * 8, width), bf16),
        ),
        in_specs=[ANY, VMEM, ANY, ANY, ANY],
        out_specs=(VMEM, ANY, ANY),
        scratch_shapes=[
            pltpu.VMEM((tok, full), bf16),
            pltpu.VMEM((full, cols), bf16),
            pltpu.VMEM((2, rows // 2, cols), bf16),
            pltpu.VMEM((tok * 16, cols - q_cols), bf16),
            pltpu.VMEM((2, tok // 2, cols - q_cols), bf16),
            pltpu.VMEM((4, deep // 2, width), bf16),
            pltpu.VMEM((depth // 8, width), bf16),
            pltpu.VMEM((deep, width), bf16),
            pltpu.VMEM((tok, cols), f32),
            pltpu.VMEM((q_cols, tok), bf16),
            pltpu.VMEM((8, tok), f32),
            pltpu.VMEM((8, tok), f32),
            pltpu.VMEM((q_cols, tok), f32),
            pltpu.SemaphoreType.DMA((6,)),
            pltpu.SemaphoreType.DMA((68,)),
            pltpu.SemaphoreType.DMA((68,)),
        ],
        compiler_params=pltpu.CompilerParams(
            collective_id=call_id, has_side_effects=True, vmem_limit_bytes=56 << 20
        ),
        name="front",
    )(tokens, gain, a, w_out, w_down)


class Gather:
    def __init__(self, buf, row, rows, split, cols, sends, base, source=None):
        z_hi, x, core, y, z_lo = place()
        ctx = ctx_of(z_hi, x, core)
        self.buf, self.cols, self.sends, self.base, self.source = buf, cols, sends, base, source
        self.y, self.z, self.other = y, z_lo, 1 - z_lo
        self.right, self.left, self.far = (y + 1) % 4, (y + 3) % 4, (y + 2) % 4
        self.to_right, self.to_left = (ctx, self.right * 2 + z_lo), (ctx, self.left * 2 + z_lo)
        self.to_z = (ctx, y * 2 + self.other)
        half, rest = split // 2, rows - split
        self.first, self.first_0, self.first_1 = (row, split), (row, half), (row + half, half)
        self.rest, self.rest_0 = (row + split, rest), (row + split, rest // 2)
        self.rest_1 = (row + split + rest // 2, rest // 2)

    def at(self, y_of, z_of, part):
        return self.buf.at[pl.ds(part[0], part[1]), pl.ds((y_of * 2 + z_of) * self.cols, self.cols)]

    def go(self, k, y_of, z_of, part, device):
        ref = self.at(y_of, z_of, part)
        self.sends.start(self.base + k, ref, ref, device)

    def got(self, k, y_of, z_of, part):
        self.sends.arrived(self.base + k, self.at(y_of, z_of, part))

    def own(self):
        for k, part, device in (
            (0, self.first, self.to_z),
            (1, self.first, self.to_right),
            (2, self.first, self.to_left),
            (3, self.rest, self.to_right),
            (4, self.rest, self.to_left),
            (5, self.rest, self.to_z),
        ):
            here = self.at(self.y, self.z, part)
            src = here if self.source is None else self.source.at[pl.ds(part[0], part[1]), :]
            self.sends.start(self.base + k, src, here, device)

    def step_a(self):
        self.got(0, self.y, self.other, self.first)
        self.go(6, self.y, self.other, self.first, self.to_right)
        self.go(7, self.y, self.other, self.first, self.to_left)

    def step_b(self):
        self.got(3, self.left, self.z, self.rest)
        self.go(10, self.left, self.z, self.rest_0, self.to_right)
        self.go(11, self.left, self.z, self.rest, self.to_z)
        self.got(4, self.right, self.z, self.rest)
        self.go(12, self.right, self.z, self.rest_1, self.to_left)
        self.go(13, self.right, self.z, self.rest, self.to_z)

    def step_c(self):
        self.got(1, self.left, self.z, self.first)
        self.go(8, self.left, self.z, self.first_0, self.to_right)
        self.got(2, self.right, self.z, self.first)
        self.go(9, self.right, self.z, self.first_1, self.to_left)

    def step_d(self):
        self.got(10, self.far, self.z, self.rest_0)
        self.go(16, self.far, self.z, self.rest_0, self.to_z)
        self.got(12, self.far, self.z, self.rest_1)
        self.go(17, self.far, self.z, self.rest_1, self.to_z)

    def step_e(self):
        self.got(6, self.left, self.other, self.first)
        self.go(14, self.left, self.other, self.first_0, self.to_right)
        self.got(7, self.right, self.other, self.first)
        self.go(15, self.right, self.other, self.first_1, self.to_left)

    def finish_near(self, use):
        self.got(5, self.y, self.other, self.rest)
        use(self.y)
        self.got(11, self.left, self.other, self.rest)
        use(self.left)
        self.got(13, self.right, self.other, self.rest)
        use(self.right)

    def finish_far(self):
        self.got(8, self.far, self.z, self.first_0)
        self.got(9, self.far, self.z, self.first_1)
        self.got(14, self.far, self.other, self.first_0)
        self.got(15, self.far, self.other, self.first_1)
        self.got(16, self.far, self.other, self.rest_0)
        self.got(17, self.far, self.other, self.rest_1)

    def finish(self):
        self.finish_near(lambda y_of: None)
        self.finish_far()


PARTS = 2


def experts_kernel(
    attended, out_cols, tokens, gain, router, chosen, slots, w_gate, w_up, down_cols,
    out, share, all_att, out_v, stream, picks, buffer, back, parts, rows, hidden, done, gate_v, up_v, down_v,
    local_sem, send_sem, recv_sem,
):
    f32, bf16 = jnp.float32, jnp.bfloat16
    z_hi, x, core, y, z_lo = place()
    me, hx = ctx_of(z_hi, x, core), y * 2 + z_lo
    tok = tokens.shape[0]
    head_cols = attended.shape[1]
    width, deep = tokens.shape[1], w_gate.shape[1]
    total = buffer.shape[0]
    chunk = total // PARTS
    slot = chunk // 16
    loads = [
        pltpu.make_async_copy(w_gate, gate_v, local_sem.at[0]),
        pltpu.make_async_copy(w_up, up_v, local_sem.at[1]),
    ]
    loads.append(pltpu.make_async_copy(down_cols, down_v, local_sem.at[2]))
    mine = pl.ds(hx * width, width)
    early = (
        pltpu.make_async_copy(attended, all_att.at[:, pl.ds(hx * head_cols, head_cols)], local_sem.at[3]),
        pltpu.make_async_copy(out_cols, out_v, local_sem.at[4]),
    )
    for copy in early:
        copy.start()
    keeps = []
    greet([((me + k) % 16, hx) for k in range(1, 16)] + [(me, (hx + k) % 8) for k in range(1, 8)])
    sends = Sends(send_sem, recv_sem)

    def spot(c, p):
        return pl.ds(c * chunk + p * slot, slot)

    def dispatch(c):
        keep = pltpu.make_async_copy(buffer.at[spot(c, me), :], rows.at[spot(c, me), mine], local_sem.at[5 + c])
        keep.start()
        keeps.append(keep)
        for k in range(1, 16):
            peer = (me + k) % 16
            sends.start(c * 15 + k - 1, buffer.at[spot(c, peer), :], rows.at[spot(c, me), mine], (peer, hx))

    def dispatched(c):
        keeps[c].wait()
        for k in range(1, 16):
            sends.arrived(c * 15 + k - 1, rows.at[spot(c, (me + 16 - k) % 16), mine])

    def give(c):
        base = PARTS * 15
        for k in range(1, 16):
            peer = (me + k) % 16
            sends.start(base + c * 15 + k - 1, done.at[spot(c, peer), :], back.at[spot(c, me), :], (peer, hx))
        keep = pltpu.make_async_copy(done.at[spot(c, me), :], back.at[spot(c, me), :], local_sem.at[5 + PARTS + c])
        keep.start()
        keeps.append(keep)

    def given(c):
        base = PARTS * 15
        keeps[PARTS + c].wait()
        for k in range(1, 16):
            sends.arrived(base + c * 15 + k - 1, back.at[spot(c, (me + 16 - k) % 16), :])

    def hide(c, n):
        step = 256
        r, f = pl.ds(c * chunk, chunk), pl.ds(n * step, step)
        gate = jnp.dot(rows[r, :], gate_v[:, f], preferred_element_type=jnp.float32)
        up = jnp.dot(rows[r, :], up_v[:, f], preferred_element_type=jnp.float32)
        spread = pl.ds(pl.multiple_of(hx * deep + n * step, step), step)
        hidden[r, spread] = (gate * jax.nn.sigmoid(gate) * up).astype(hidden.dtype)

    def lower(c):
        r = pl.ds(c * chunk, chunk)
        for at, step in ((0, 256), (256, 256), (512, 128)):
            f = pl.ds(at, step)
            done[r, f] = jnp.dot(hidden[r, :], down_v[:, f], preferred_element_type=jnp.float32).astype(done.dtype)

    base = PARTS * 30
    split = chunk * 9 // 16 // 32 * 32
    row_gathers = [Gather(rows, c * chunk, chunk, split, width, sends, base + 18 * c) for c in range(PARTS)]
    base += 18 * PARTS
    hid_gathers = [Gather(hidden, c * chunk, chunk, split, deep, sends, base + 18 * c) for c in range(PARTS)]
    r0, r1 = row_gathers
    h0, h1 = hid_gathers

    base += 18 * PARTS
    att = Gather(all_att, 0, tok, tok * 9 // 16 // 32 * 32, head_cols, sends, base, attended)
    base += 18
    att.own()
    for load in loads:
        load.start()
    row_slot = lax.broadcasted_iota(jnp.int32, (total, tok), 0)
    picks[...] = jnp.where(row_slot == slots[...], 1.0, 0.0).astype(bf16)
    att.step_a()
    att.step_b()
    att.step_c()
    att.step_d()
    att.step_e()
    for copy in early:
        copy.wait()
    share[...] = tokens[...].astype(f32)

    def project(y_of):
        at = pl.ds(pl.multiple_of(y_of * 2 * head_cols, 2 * head_cols), 2 * head_cols)
        share[...] += jnp.dot(all_att[:, at], out_v[at, :], preferred_element_type=f32)

    att.finish_near(project)
    att.finish_far()
    project(att.far)
    stream[...] = share[...].astype(bf16)
    floats = stream[...].astype(f32)
    logits = jnp.dot((floats * gain[...]).astype(bf16), router[...], preferred_element_type=f32)
    lane = lax.broadcasted_iota(jnp.int32, logits.shape, 1)
    logit = jnp.sum(jnp.where(lane == chosen[...], logits, 0.0), axis=1, keepdims=True)
    square = jnp.sum(floats * floats, axis=1, keepdims=True)
    parts[hx] = jnp.where(lane == 0, square, jnp.where(lane == 1, logit, 0.0)).T[:8, :]
    for k in range(1, 8):
        sends.start(base + k - 1, parts.at[hx], parts.at[hx], (me, (hx + k) % 8))
    for k in range(1, 8):
        sends.arrived(base + k - 1, parts.at[(hx + 8 - k) % 8])
    both = jnp.sum(parts[...], axis=0)
    inverse = lax.rsqrt(both[0:1, :] / rows.shape[1] + epsilon)
    score = jax.nn.sigmoid(both[1:2, :] * inverse)
    line = lax.broadcasted_iota(jnp.int32, (128, tok), 0)
    column = jnp.where(line == 0, inverse, jnp.where(line == 1, score, 0.0)).T
    normed = (stream[...].astype(f32) * column[:, 0:1] * gain[...]).astype(bf16)
    routed = (normed.astype(f32) * column[:, 1:2]).astype(bf16)
    for c in range(PARTS):
        r = pl.ds(c * chunk, chunk)
        buffer[r, :] = jnp.dot(picks[r, :], routed, preferred_element_type=f32).astype(bf16)
        dispatch(c)
    dispatched(0)
    r0.own()
    r0.step_a()
    r0.step_b()
    dispatched(1)
    r1.own()
    r0.step_c()
    r0.step_d()
    r0.step_e()
    r1.step_a()
    r1.step_b()
    r0.finish()
    for load in loads:
        load.wait()
    hide(0, 0)
    r1.step_c()
    r1.step_d()
    hide(0, 1)
    r1.step_e()
    h0.own()
    r1.finish()
    hide(1, 0)
    h0.step_a()
    h0.step_b()
    hide(1, 1)
    h0.step_c()
    h1.own()
    h0.step_d()
    h0.step_e()
    h1.step_a()
    h1.step_b()
    h0.finish()
    lower(0)
    h1.step_c()
    h1.step_d()
    give(0)
    h1.step_e()
    h1.finish()
    lower(1)

    def placed(c):
        r = pl.ds(c * chunk, chunk)
        return lax.dot_general(picks[r, :], back[r, :], (((0,), (0,)), ((), ())), preferred_element_type=f32)

    given(0)
    give(1)
    found = placed(0)
    given(1)
    found = (found + placed(1)).astype(bf16).astype(f32)
    out[...] = (stream[...].astype(f32) + found).astype(out.dtype)
    sends.drain()


def run_experts(attended, out_cols, tokens, gain, router, chosen, slots, total, w_gate, w_up, down_cols, call_id):
    tok, width = tokens.shape
    full, deep = w_gate.shape
    bf16 = jnp.bfloat16
    copies = PARTS * 66 + 25
    return pl.pallas_call(
        experts_kernel,
        out_shape=jax.ShapeDtypeStruct((tok, width), bf16),
        in_specs=[ANY, ANY, VMEM, VMEM, VMEM, VMEM, VMEM, ANY, ANY, ANY],
        out_specs=VMEM,
        scratch_shapes=[
            pltpu.VMEM((tok, width), jnp.float32),
            pltpu.VMEM((tok, attended.shape[1] * 8), bf16),
            pltpu.VMEM(out_cols.shape, bf16),
            pltpu.VMEM((tok, width), bf16),
            pltpu.VMEM((total, tok), bf16),
            pltpu.VMEM((total, width), bf16),
            pltpu.VMEM((total, width), bf16),
            pltpu.VMEM((8, 8, tok), jnp.float32),
            pltpu.VMEM((total, full), bf16),
            pltpu.VMEM((total, deep * 8), bf16),
            pltpu.VMEM((total, width), bf16),
            pltpu.VMEM((full, deep), bf16),
            pltpu.VMEM((full, deep), bf16),
            pltpu.VMEM((deep * 8, width), bf16),
            pltpu.SemaphoreType.DMA((5 + 2 * PARTS,)),
            pltpu.SemaphoreType.DMA((copies,)),
            pltpu.SemaphoreType.DMA((copies,)),
        ],
        compiler_params=pltpu.CompilerParams(
            collective_id=call_id, has_side_effects=True, vmem_limit_bytes=63 << 20
        ),
        name="experts",
    )(attended, out_cols, tokens, gain, router, chosen, slots, w_gate, w_up, down_cols)


def body(tokens, attn_gain, ffn_gain, w_query, w_key, w_value, w_out, w_router, routes, w_gate, w_up, w_down):
    f32, bf16 = jnp.float32, jnp.bfloat16
    hx = lax.axis_index("hx")
    tok_rows, full_width = tokens.shape
    width = full_width // 8

    w_down = w_down[0]

    qkv = jnp.concatenate((w_query, w_key, w_value), axis=1)
    attended, out_cols, down_cols = run_front(
        tokens, attn_gain.astype(f32)[None, :], qkv, w_out, w_down, w_query.shape[1], 2
    )
    own_tokens = lax.dynamic_slice_in_dim(tokens, hx * width, width, 1)
    own_gain = lax.dynamic_slice_in_dim(ffn_gain, hx * width, width, 0).astype(f32)[None, :]
    own_router = lax.dynamic_slice_in_dim(w_router, hx * width, width, 0)
    experts = w_router.shape[1]
    own_router = jnp.pad(own_router, ((0, 0), (0, 128 - experts)))
    capacity = tok_rows // 8
    chosen = routes[:, 0]
    onehot = chosen[:, None] == jnp.arange(experts, dtype=jnp.int32)[None, :]
    counts = jnp.cumsum(onehot.astype(jnp.int32), axis=0)
    position = jnp.sum(jnp.where(onehot, counts, 0), axis=-1) - 1
    slots = capacity // PARTS
    slot = position // slots * (experts * slots) + chosen * slots + position % slots
    return run_experts(
        attended, out_cols.reshape(-1, width), own_tokens, own_gain, own_router, routes, slot[None, :], experts * capacity,
        w_gate[0], w_up[0], down_cols, 6,
    )


def solution(mesh):
    in_specs = (
        P("ctx", None),
        P(),
        P(),
        P("ctx", "hx"),
        P("ctx", "hx"),
        P("ctx", "hx"),
        P("hx", None),
        P(),
        P("ctx", None),
        P("ctx", None, "hx"),
        P("ctx", None, "hx"),
        P("ctx", "hx", None),
    )
    return jax.shard_map(body, mesh=mesh, in_specs=in_specs, out_specs=P("ctx", "hx"), check_vma=False)
```

time: 906 us -> 327 us (0.36)
  waiting for transfers between devices: 696 us -> 0 us
  Pallas kernels: 0 us -> 312 us
  matrix products: 83 us -> 0 us
  local copies, waits for them, and re-layouts: 40.8 us -> 7.19 us
  blocking collectives: 27.2 us -> 0 us
  other arithmetic: 34.8 us -> 7.83 us
  between operations: 13.8 us -> 0.03 us
    all_gather x4 -> x0, waiting for transfers between devices: 429 us -> none  [the longest x1 204 us: body(): joined = lax.all_gather(arrived, HX, axis=3, tiled=True)]
    pallas_call x0 -> x2, Pallas kernels: none -> 312 us  [the longest x1 198 us: run_experts(): pl.pallas_call(experts_kernel, out_shape=jax.ShapeDtypeStruct((tok, width...]
    unnamed x9 -> x0, waiting for transfers between devices: 148 us -> none
    reduce_scatter x1 -> x0, waiting for transfers between devices: 98.7 us -> none  [summed_rows(): nearer = lax.psum_scatter(x, axes[0], scatter_dimension=dim, tiled=True)]
    dot_general x24 -> x0, matrix products: 83 us -> none  [the longest x8 22.3 us: attend(): jnp.einsum('tkgs,skd->tkgd', weights.astype(jnp.bfloat16), value_heads, p...]
    unnamed x25 -> x5, local copies, waits for them, and re-layouts: 34.6 us -> 3.69 us
    all_to_all x1 -> x0, blocking collectives: 27.2 us -> none  [body(): lax.all_to_all(buffer, 'ctx', split_axis=0, concat_axis=0, tiled=True)]
    all_to_all x1 -> x0, waiting for transfers between devices: 20.1 us -> none  [body(): lax.all_to_all(reduced, 'ctx', split_axis=0, concat_axis=0, tiled=True)]
  transfers between devices with their start and end apart: 8 -> 0, of which waited for: 8 -> 0; matrix products, arithmetic and copies ran while one was open for 1% -> 0% of each run, Pallas kernels for 0% -> 0%
where the time goes in v4:
time: 327 us
  Pallas kernels  312 us (95%)
  other arithmetic  7.83 us (2%)
  local copies, waits for them, and re-layouts  7.19 us (2%)
    pallas_call x1, Pallas kernels, run_experts(): pl.pallas_call(experts_kernel, out_shape=jax.ShapeDtypeStruct((tok, width...  198 us
    pallas_call x1, Pallas kernels, run_front(): pl.pallas_call(front_kernel, out_shape=(jax.ShapeDtypeStruct((tok, q_cols...  114 us

profile of v4, /device:TPU:1, one launch (start us, length us, event | category | flops | bytes accessed | tf_op | source)
XLA Modules:
  0.0 326.9 jit_solution(6619992911707236492)
XLA Ops:
  0.0 0.0 copy-start
  0.0 0.8 dynamic-slice_convert_fusion
  0.8 0.6 reshape.116.gain
  1.4 1.3 broadcast_in_dim.21
  2.7 0.0 copy-done
  2.7 0.7 fusion.2
  3.4 1.1 reduce-window.6
  4.5 0.2 slice_reduce_fusion
  4.8 0.8 fusion.1
  5.6 1.2 fusion.3.slots
  6.8 0.2 copy.18
  7.0 0.7 pad.4.router
  7.7 1.5 copy.17.chosen
  9.2 1.8 pad_maximum_fusion.a
  11.1 2.0 constant_dynamic-slice_fusion.1.tokens
  13.0 114.0 %front.1 = (bf16[512,384]{1,0:T(8,128)(2,1)}, bf16[8,8,48,640]{3,2,1,0:T(8,128)(2,1)}, bf16[4096,640]{1,0:T(8,128)(2,1)}) custom-call(bf16[512,5120]{1,0:T(8,128)(2,1)} %tokens.1, f32[1,5120]{1,0:T(1,128)} %bitcast.31, bf16[320,640]{1,0:T(8,128)(2,1)} %pad_maximum_fusion.a, bf16[384,5120]{1,0:T(8,128)(2,1)} %w_out.1, bf16[512,5120]{1,0:T(8,128)(2,1)} %bitcast.27), custom_call_target="tpu_custom_call" | custom-call | tf_op jit(solution)/shard_map/front/pallas_call | solution.py:392
  127.1 197.8 %experts.1 = bf16[512,640]{1,0:T(8,128)(2,1)} custom-call(bf16[512,384]{1,0:T(8,128)(2,1)} %get-tuple-element.8.attended, bf16[3072,640]{1,0:T(8,128)(2,1)} %bitcast.30, bf16[512,640]{1,0:T(8,128)(2,1)} %constant_dynamic-slice_fusion.1.tokens, f32[1,640]{1,0:T(1,128)} %reshape.116.gain, bf16[640,128]{1,0:T(8,128)(2,1)} %pad.4.router, s32[512,1]{1,0:T(8,128)} %copy.17.chosen, ...), custom_call_target="tpu_custom_call" | custom-call | tf_op jit(solution)/shard_map/experts/pallas_call | solution.py:705
  324.9 2.0 copy.22
  (4 shorter events, 0.0 us)
Async XLA Ops:
  0.0 2.7 copy-start

commit v5 on v4

--- a/solution.py
+++ b/solution.py
@@ -512,7 +512,7 @@
         self.finish_far()
 
 
-PARTS = 2
+PARTS = 4
 
 
 def experts_kernel(
@@ -576,13 +576,19 @@
         for k in range(1, 16):
             sends.arrived(base + c * 15 + k - 1, back.at[spot(c, (me + 16 - k) % 16), :])
 
-    def hide(c, n):
+    def hide(c):
         step = 256
-        r, f = pl.ds(c * chunk, chunk), pl.ds(n * step, step)
-        gate = jnp.dot(rows[r, :], gate_v[:, f], preferred_element_type=jnp.float32)
-        up = jnp.dot(rows[r, :], up_v[:, f], preferred_element_type=jnp.float32)
-        spread = pl.ds(pl.multiple_of(hx * deep + n * step, step), step)
-        hidden[r, spread] = (gate * jax.nn.sigmoid(gate) * up).astype(hidden.dtype)
+        r = pl.ds(c * chunk, chunk)
+
+        def some(n, carry):
+            f = pl.ds(pl.multiple_of(n * step, step), step)
+            gate = jnp.dot(rows[r, :], gate_v[:, f], preferred_element_type=jnp.float32)
+            up = jnp.dot(rows[r, :], up_v[:, f], preferred_element_type=jnp.float32)
+            spread = pl.ds(pl.multiple_of(hx * deep + n * step, step), step)
+            hidden[r, spread] = (gate * jax.nn.sigmoid(gate) * up).astype(hidden.dtype)
+            return carry
+
+        lax.fori_loop(0, deep // step, some, 0)
 
     def lower(c):
         r = pl.ds(c * chunk, chunk)
@@ -591,12 +597,12 @@
             done[r, f] = jnp.dot(hidden[r, :], down_v[:, f], preferred_element_type=jnp.float32).astype(done.dtype)
 
     base = PARTS * 30
-    split = chunk * 9 // 16 // 32 * 32
-    row_gathers = [Gather(rows, c * chunk, chunk, split, width, sends, base + 18 * c) for c in range(PARTS)]
+    splits = [chunk * (10 - 2 * (c % 2)) // 16 // 32 * 32 for c in range(PARTS)]
+    row_gathers = [Gather(rows, c * chunk, chunk, splits[c], width, sends, base + 18 * c) for c in range(PARTS)]
     base += 18 * PARTS
-    hid_gathers = [Gather(hidden, c * chunk, chunk, split, deep, sends, base + 18 * c) for c in range(PARTS)]
-    r0, r1 = row_gathers
-    h0, h1 = hid_gathers
+    hid_gathers = [Gather(hidden, c * chunk, chunk, splits[c], deep, sends, base + 18 * c) for c in range(PARTS)]
+    r0, r1, r2, r3 = row_gathers
+    h0, h1, h2, h3 = hid_gathers
 
     base += 18 * PARTS
     att = Gather(all_att, 0, tok, tok * 9 // 16 // 32 * 32, head_cols, sends, base, attended)
@@ -644,55 +650,76 @@
         r = pl.ds(c * chunk, chunk)
         buffer[r, :] = jnp.dot(picks[r, :], routed, preferred_element_type=f32).astype(bf16)
         dispatch(c)
+    def tail(g):
+        g.step_c()
+        g.step_d()
+        g.step_e()
+
+    def head(g):
+        g.step_a()
+        g.step_b()
+
     dispatched(0)
     r0.own()
-    r0.step_a()
-    r0.step_b()
+    head(r0)
     dispatched(1)
     r1.own()
-    r0.step_c()
-    r0.step_d()
-    r0.step_e()
-    r1.step_a()
-    r1.step_b()
+    tail(r0)
+    head(r1)
+    dispatched(2)
+    r2.own()
     r0.finish()
+    tail(r1)
+    head(r2)
+    dispatched(3)
+    r3.own()
     for load in loads:
         load.wait()
-    hide(0, 0)
-    r1.step_c()
-    r1.step_d()
-    hide(0, 1)
-    r1.step_e()
+    hide(0)
+    r1.finish()
+    tail(r2)
+    head(r3)
     h0.own()
-    r1.finish()
-    hide(1, 0)
-    h0.step_a()
-    h0.step_b()
-    hide(1, 1)
-    h0.step_c()
+    hide(1)
+    tail(r3)
+    r2.finish()
+    head(h0)
     h1.own()
-    h0.step_d()
-    h0.step_e()
-    h1.step_a()
-    h1.step_b()
+    hide(2)
+    tail(h0)
+    r3.finish()
+    head(h1)
+    h2.own()
+    hide(3)
+    tail(h1)
     h0.finish()
+    head(h2)
+    h3.own()
     lower(0)
-    h1.step_c()
-    h1.step_d()
+    tail(h2)
+    h1.finish()
     give(0)
-    h1.step_e()
-    h1.finish()
+    head(h3)
     lower(1)
+    tail(h3)
+    h2.finish()
+    give(1)
+    lower(2)
+    h3.finish()
+    give(2)
+    lower(3)
 
     def placed(c):
         r = pl.ds(c * chunk, chunk)
         return lax.dot_general(picks[r, :], back[r, :], (((0,), (0,)), ((), ())), preferred_element_type=f32)
 
     given(0)
-    give(1)
     found = placed(0)
-    given(1)
-    found = (found + placed(1)).astype(bf16).astype(f32)
+    give(3)
+    for c in range(1, PARTS):
+        given(c)
+        found = found + placed(c)
+    found = found.astype(bf16).astype(f32)
     out[...] = (stream[...].astype(f32) + found).astype(out.dtype)
     sends.drain()
 

time: 327 us -> 323 us (0.988)
  Pallas kernels: 312 us -> 307 us
    pallas_call x1, Pallas kernels: 198 us -> 193 us  [run_experts(): pl.pallas_call(experts_kernel, out_shape=jax.ShapeDtypeStruct((tok, width...]
where the time goes in v5:
time: 323 us; the launch traced here: 322 us
  Pallas kernels  307 us (95%)
  other arithmetic  7.83 us (2%)
  local copies, waits for them, and re-layouts  7.19 us (2%)
    pallas_call x1, Pallas kernels, run_experts(): pl.pallas_call(experts_kernel, out_shape=jax.ShapeDtypeStruct((tok, width...  193 us
    pallas_call x1, Pallas kernels, run_front(): pl.pallas_call(front_kernel, out_shape=(jax.ShapeDtypeStruct((tok, q_cols...  114 us

profile of v5, /device:TPU:1, one launch (start us, length us, event | category | flops | bytes accessed | tf_op | source)
XLA Modules:
  0.0 322.3 jit_solution(18373596423093381327)
XLA Ops:
  0.0 0.0 copy-start
  0.0 0.8 dynamic-slice_convert_fusion
  0.8 0.6 reshape.116.gain
  1.4 1.3 broadcast_in_dim.21
  2.7 0.0 copy-done
  2.7 0.7 fusion.2
  3.4 1.1 reduce-window.6
  4.5 0.2 slice_reduce_fusion
  4.8 0.8 fusion.1
  5.6 1.2 fusion.3.slots
  6.8 0.2 copy.18
  7.0 0.7 pad.4.router
  7.7 1.5 copy.17.chosen
  9.2 1.8 pad_maximum_fusion.a
  11.1 2.0 constant_dynamic-slice_fusion.1.tokens
  13.0 114.0 %front.1 = (bf16[512,384]{1,0:T(8,128)(2,1)}, bf16[8,8,48,640]{3,2,1,0:T(8,128)(2,1)}, bf16[4096,640]{1,0:T(8,128)(2,1)}) custom-call(bf16[512,5120]{1,0:T(8,128)(2,1)} %tokens.1, f32[1,5120]{1,0:T(1,128)} %bitcast.31, bf16[320,640]{1,0:T(8,128)(2,1)} %pad_maximum_fusion.a, bf16[384,5120]{1,0:T(8,128)(2,1)} %w_out.1, bf16[512,5120]{1,0:T(8,128)(2,1)} %bitcast.27), custom_call_target="tpu_custom_call" | custom-call | tf_op jit(solution)/shard_map/front/pallas_call | solution.py:392
  127.1 193.2 %experts.1 = bf16[512,640]{1,0:T(8,128)(2,1)} custom-call(bf16[512,384]{1,0:T(8,128)(2,1)} %get-tuple-element.8.attended, bf16[3072,640]{1,0:T(8,128)(2,1)} %bitcast.30, bf16[512,640]{1,0:T(8,128)(2,1)} %constant_dynamic-slice_fusion.1.tokens, f32[1,640]{1,0:T(1,128)} %reshape.116.gain, bf16[640,128]{1,0:T(8,128)(2,1)} %pad.4.router, s32[512,1]{1,0:T(8,128)} %copy.17.chosen, ...), custom_call_target="tpu_custom_call" | custom-call | tf_op jit(solution)/shard_map/experts/pallas_call | solution.py:732
  320.3 2.0 copy.22
  (4 shorter events, 0.0 us)
Async XLA Ops:
  0.0 2.7 copy-start

commit v6 on v5

--- a/solution.py
+++ b/solution.py
@@ -517,7 +517,7 @@
 
 def experts_kernel(
     attended, out_cols, tokens, gain, router, chosen, slots, w_gate, w_up, down_cols,
-    out, share, all_att, out_v, stream, picks, buffer, back, parts, rows, hidden, done, gate_v, up_v, down_v,
+    out, own_tokens, share, all_att, out_v, stream, picks, buffer, back, parts, rows, hidden, done, gate_v, up_v, down_v,
     local_sem, send_sem, recv_sem,
 ):
     f32, bf16 = jnp.float32, jnp.bfloat16
@@ -525,7 +525,7 @@
     me, hx = ctx_of(z_hi, x, core), y * 2 + z_lo
     tok = tokens.shape[0]
     head_cols = attended.shape[1]
-    width, deep = tokens.shape[1], w_gate.shape[1]
+    width, deep = out.shape[1], w_gate.shape[1]
     total = buffer.shape[0]
     chunk = total // PARTS
     slot = chunk // 16
@@ -538,6 +538,7 @@
     early = (
         pltpu.make_async_copy(attended, all_att.at[:, pl.ds(hx * head_cols, head_cols)], local_sem.at[3]),
         pltpu.make_async_copy(out_cols, out_v, local_sem.at[4]),
+        pltpu.make_async_copy(tokens.at[:, mine], own_tokens, local_sem.at[5 + 2 * PARTS]),
     )
     for copy in early:
         copy.start()
@@ -619,7 +620,7 @@
     att.step_e()
     for copy in early:
         copy.wait()
-    share[...] = tokens[...].astype(f32)
+    share[...] = own_tokens[...].astype(f32)
 
     def project(y_of):
         at = pl.ds(pl.multiple_of(y_of * 2 * head_cols, 2 * head_cols), 2 * head_cols)
@@ -725,16 +726,17 @@
 
 
 def run_experts(attended, out_cols, tokens, gain, router, chosen, slots, total, w_gate, w_up, down_cols, call_id):
-    tok, width = tokens.shape
-    full, deep = w_gate.shape
+    tok, full = tokens.shape
+    deep, width = w_gate.shape[1], full // 8
     bf16 = jnp.bfloat16
     copies = PARTS * 66 + 25
     return pl.pallas_call(
         experts_kernel,
         out_shape=jax.ShapeDtypeStruct((tok, width), bf16),
-        in_specs=[ANY, ANY, VMEM, VMEM, VMEM, VMEM, VMEM, ANY, ANY, ANY],
+        in_specs=[ANY, ANY, ANY, VMEM, VMEM, VMEM, VMEM, ANY, ANY, ANY],
         out_specs=VMEM,
         scratch_shapes=[
+            pltpu.VMEM((tok, width), bf16),
             pltpu.VMEM((tok, width), jnp.float32),
             pltpu.VMEM((tok, attended.shape[1] * 8), bf16),
             pltpu.VMEM(out_cols.shape, bf16),
@@ -749,7 +751,7 @@
             pltpu.VMEM((full, deep), bf16),
             pltpu.VMEM((full, deep), bf16),
             pltpu.VMEM((deep * 8, width), bf16),
-            pltpu.SemaphoreType.DMA((5 + 2 * PARTS,)),
+            pltpu.SemaphoreType.DMA((6 + 2 * PARTS,)),
             pltpu.SemaphoreType.DMA((copies,)),
             pltpu.SemaphoreType.DMA((copies,)),
         ],
@@ -772,7 +774,6 @@
     attended, out_cols, down_cols = run_front(
         tokens, attn_gain.astype(f32)[None, :], qkv, w_out, w_down, w_query.shape[1], 2
     )
-    own_tokens = lax.dynamic_slice_in_dim(tokens, hx * width, width, 1)
     own_gain = lax.dynamic_slice_in_dim(ffn_gain, hx * width, width, 0).astype(f32)[None, :]
     own_router = lax.dynamic_slice_in_dim(w_router, hx * width, width, 0)
     experts = w_router.shape[1]
@@ -785,7 +786,7 @@
     slots = capacity // PARTS
     slot = position // slots * (experts * slots) + chosen * slots + position % slots
     return run_experts(
-        attended, out_cols.reshape(-1, width), own_tokens, own_gain, own_router, routes, slot[None, :], experts * capacity,
+        attended, out_cols.reshape(-1, width), tokens, own_gain, own_router, routes, slot[None, :], experts * capacity,
         w_gate[0], w_up[0], down_cols, 6,
     )
 

time: 323 us -> 321 us (level)
  no operation moved by 1% of the time
where the time goes in v6:
time: 321 us; the launch traced here: 320 us
  Pallas kernels  307 us (96%)
  other arithmetic  7.79 us (2%)
  local copies, waits for them, and re-layouts  5.21 us (2%)
    pallas_call x1, Pallas kernels, run_experts(): pl.pallas_call(experts_kernel, out_shape=jax.ShapeDtypeStruct((tok, width...  193 us
    pallas_call x1, Pallas kernels, run_front(): pl.pallas_call(front_kernel, out_shape=(jax.ShapeDtypeStruct((tok, q_cols...  114 us

profile of v6, /device:TPU:1, one launch (start us, length us, event | category | flops | bytes accessed | tf_op | source)
XLA Modules:
  0.0 320.1 jit_solution(7158255954969624889)
XLA Ops:
  0.0 0.0 copy-start
  0.0 0.8 dynamic-slice_convert_fusion
  0.8 0.6 reshape.116.gain
  1.4 0.0 copy-done
  1.4 1.3 broadcast_in_dim.21
  2.7 0.7 fusion.2
  3.4 1.1 reduce-window.6
  4.5 0.2 slice_reduce_fusion
  4.8 0.8 fusion.1
  5.6 1.2 fusion.3.slots
  6.8 0.2 copy.18
  7.0 0.7 pad.4.router
  7.7 1.5 copy.17.chosen
  9.2 1.8 pad_maximum_fusion.a
  11.0 114.0 %front.1 = (bf16[512,384]{1,0:T(8,128)(2,1)}, bf16[8,8,48,640]{3,2,1,0:T(8,128)(2,1)}, bf16[4096,640]{1,0:T(8,128)(2,1)}) custom-call(bf16[512,5120]{1,0:T(8,128)(2,1)} %tokens.3, f32[1,5120]{1,0:T(1,128)} %bitcast.31, bf16[320,640]{1,0:T(8,128)(2,1)} %pad_maximum_fusion.a, bf16[384,5120]{1,0:T(8,128)(2,1)} %w_out.1, bf16[512,5120]{1,0:T(8,128)(2,1)} %bitcast.27), custom_call_target="tpu_custom_call" | custom-call | tf_op jit(solution)/shard_map/front/pallas_call | solution.py:392
  125.1 193.1 %experts.1 = bf16[512,640]{1,0:T(8,128)(2,1)} custom-call(bf16[512,384]{1,0:T(8,128)(2,1)} %get-tuple-element.8.attended, bf16[3072,640]{1,0:T(8,128)(2,1)} %bitcast.30, bf16[512,5120]{1,0:T(8,128)(2,1)} %tokens.3, f32[1,640]{1,0:T(1,128)} %reshape.116.gain, bf16[640,128]{1,0:T(8,128)(2,1)} %pad.4.router, s32[512,1]{1,0:T(8,128)} %copy.17.chosen, ...), custom_call_target="tpu_custom_call" | custom-call | tf_op jit(solution)/shard_map/experts/pallas_call | solution.py:733
  318.1 2.0 copy.22
  (4 shorter events, 0.0 us)
Async XLA Ops:
  0.0 1.4 copy-start
